TPU v7x, 512 devices: a whole 4x8x8 slice. The times are simulated.
512 devices in a mesh: dp: 32 (over x, z), var: 16 (over y, core).
Axes of the slice: x: 4, y: 8, z: 8, core: 2. Of those that a mesh axis runs over, the one named last changes fastest.
Arguments:
- pixels: bfloat16 [32, 96, 4, 256], P('dp', 'var'), may hold values from -6 to 6
- var_ids: int32 [32, 96], P('dp', 'var'), may hold values from 0 to 90, as said below
- counts: int32 [32], P('dp'), may hold values from 3 to 91, as said below
- patch_weight: bfloat16 [91, 4, 1024], replicated, may hold values from -3 to 3
- var_embed: bfloat16 [91, 1024], replicated, may hold values from -5 to 5
- norm_gain: float32 [1024], replicated, may hold values from 0.1 to 1.9
- norm_bias: float32 [1024], replicated, may hold values from -3 to 3
- key_weight: bfloat16 [1024, 1024], P('dp'), may hold values from -0.1875 to 0.1875
- value_weight: bfloat16 [1024, 1024], P('dp'), may hold values from -0.1875 to 0.1875
- query: float32 [16, 64], replicated, may hold values from -200 to 200
- out_weight: bfloat16 [1024, 1024], replicated, may hold values from -0.1875 to 0.1875
Outputs:
- aggregated: bfloat16 [32, 256, 1024], P('dp', 'var')
Inputs may be any that keep to these rules, and one draw needn't show every extreme that they name: `var_ids`: in each sample the ids of slots below its count are distinct; slots at or past the count are padding with arbitrary ids. `counts`: some sample has exactly min(91, 96) live slots and some has exactly 3.
All inputs are finite; a program needn't handle non-finite values.
Results may differ from a plain program's by a relative error of at most 0.018.
Values may be sent and summed in bfloat16 or wider, within the bound.
No kernel may reach another device: no remote copies, remote signals or barrier semaphores. Data moves between devices by JAX's collectives and lax.ppermute only.
A program may use at most 64 MiB of HBM per device.

v0:
```python
import math

import jax
import jax.numpy as jnp
from jax import lax
from jax.sharding import Mesh
from jax.sharding import PartitionSpec as P

DP = ("dp_0", "dp_1")


def laid_out(pieces, dim):
    lengths = list(pieces.shape[1:])
    lengths[dim] *= pieces.shape[0]
    return jnp.moveaxis(pieces, 0, dim).reshape(lengths)


def sent_to_all(x, axis):
    copies = jnp.broadcast_to(x, (lax.axis_size(axis), *x.shape))
    return lax.all_to_all(copies, axis, split_axis=0, concat_axis=0, tiled=True)


def collect(x, axis, dim):
    return laid_out(sent_to_all(x, axis), dim)


def gather_in_order(x, axes, order):
    pieces = x
    for k in order:
        pieces = lax.all_gather(pieces, axes[k])
    done = order[::-1]
    back = [done.index(k) for k in range(len(axes))]
    pieces = pieces.transpose(*back, *range(len(axes), pieces.ndim))
    return pieces.reshape(-1, *x.shape)


def gathered_by_axis(x, axes, order, dim):
    return laid_out(gather_in_order(x, axes, order), dim)


def of_everyone(x, axis):
    return sent_to_all(x, axis).max(axis=0)


def cut_along(x, dim, length):
    lengths = x.shape
    pieces = x.reshape(*lengths[:dim], length, lengths[dim] // length, *lengths[dim + 1 :])
    return jnp.moveaxis(pieces, dim, 0)


def sum_at_owner(x, axis, dim):
    length = lax.axis_size(axis)
    pieces = lax.all_to_all(cut_along(x, dim, length), axis, 0, 0, tiled=True)
    return jnp.sum(pieces.astype(jnp.float32), axis=0)


def in_one_piece(arrays, axis, dim, along):
    ends, at = ([], 0)
    for a in arrays[:-1]:
        at += a.shape[along]
        ends.append(at)
    both = jnp.concatenate(arrays, axis=along)
    return tuple(jnp.split(sum_at_owner(both, axis, dim), ends, axis=along))


def on_device(
    pixels,
    var_ids,
    counts,
    patch_weight,
    var_embed,
    norm_gain,
    norm_bias,
    key_weight,
    value_weight,
    query,
    out_weight,
):
    slots = pixels.shape[1]
    patches = pixels.shape[3]
    width = out_weight.shape[0]
    heads = query.shape[0]
    head_size = query.shape[1]
    ids = var_ids[0]
    table = patch_weight[ids]
    embedded = jnp.einsum("skp,skd->spd", pixels[0], table, preferred_element_type=jnp.float32)
    embedded = embedded + var_embed[ids].astype(jnp.float32)[:, None, :]
    center = embedded - jnp.mean(embedded, axis=-1, keepdims=True)
    spread = jnp.mean(center * center, axis=-1, keepdims=True)
    normed = (center * lax.rsqrt(spread + 1e-05) * norm_gain + norm_bias).astype(jnp.bfloat16)
    flat = normed.reshape(slots * patches, width)
    local_fold = jnp.einsum(
        "jhe,he->jh",
        key_weight.astype(jnp.float32).reshape(-1, heads, head_size),
        query,
        precision=lax.Precision.HIGHEST,
    )
    folded = collect(local_fold, DP, 0)
    values = jnp.dot(
        flat, gathered_by_axis(value_weight, DP, (0, 1), 0), preferred_element_type=jnp.float32
    )
    scores = jnp.dot(flat.astype(jnp.float32), folded, precision=lax.Precision.HIGHEST)
    scores = (scores * (1.0 / math.sqrt(head_size))).reshape(slots, patches, heads)
    first_slot = lax.axis_index("var") * slots
    live = (first_slot + jnp.arange(slots, dtype=jnp.int32) < counts[0])[:, None, None]
    scores = jnp.where(live, scores, jnp.float32(-1e30))
    values = values.astype(jnp.bfloat16).reshape(slots, patches, width)
    peak = of_everyone(jnp.max(scores, axis=0), "var")
    expo = jnp.exp(scores - peak)
    part_numer = jnp.einsum(
        "sph,sphe->phe",
        expo.astype(jnp.bfloat16),
        values.reshape(slots, patches, heads, head_size),
        preferred_element_type=jnp.float32,
    )
    numer, total = in_one_piece(
        (
            part_numer.reshape(patches, width).astype(jnp.bfloat16),
            jnp.sum(expo, axis=0).astype(jnp.bfloat16),
        ),
        "var",
        0,
        1,
    )
    numer = numer.reshape(-1, heads, head_size)
    mixed = (numer / total[:, :, None]).reshape(-1, width).astype(jnp.bfloat16)
    return jnp.dot(mixed, out_weight, preferred_element_type=jnp.float32).astype(jnp.bfloat16)[None]


def solution(mesh):
    torus = Mesh(mesh.devices.reshape(4, 8, mesh.shape["var"]), ("dp_0", "dp_1", "var"))
    return jax.shard_map(
        on_device,
        mesh=torus,
        in_specs=(
            P(DP, "var", None, None),
            P(DP, "var"),
            P(DP),
            P(),
            P(),
            P(),
            P(),
            P(DP, None),
            P(DP, None),
            P(),
            P(),
        ),
        out_specs=P(DP, "var", None),
        check_vma=False,
    )
```

profile of v0, /device:TPU:1, one launch (start us, length us, event | category | flops | bytes accessed | tf_op | source)
XLA Modules:
  0.0 134.2 jit_solution(17475279565227859906)
XLA Ops:
  6.5 12.9 %all-gather = bf16[128,1024]{1,0:T(8,128)(2,1)} all-gather(bf16[32,1024]{1,0:T(8,128)(2,1)} %param.19), channel_id=2, replica_groups=mesh['dp_0'=4,'dp_1'=8,'var'=16] {'dp_0'}, dimensions={0}, use_global_device_ids=true | all-gather | bytes 327680 | tf_op jit(solution)/shard_map/all_gather | solution.py:30
  19.5 1.0 reshape.76
  20.5 1.0 fusion.1
  21.5 0.8 reshape.101
  22.3 11.0 %all-to-all-start = ((f32[32,1,512]{2,1,0:T(1,128)}), f32[32,1,512]{2,1,0:T(1,128)S(1)}, u32[]{:S(2)}, u32[]{:S(2)}) async-start(f32[32,1,512]{2,1,0:T(1,128)} %reshape.101), calls=%async_computation | async-start | bytes 131072 | tf_op jit(solution)/shard_map/all_to_all | solution.py:20
  33.3 0.7 fusion.11
  34.0 1.5 %gather_fusion.1 = bf16[6,1024]{1,0:T(8,128)(2,1)S(1)} fusion(bf16[91,1024]{1,0:T(8,128)(2,1)} %param.15, s32[1024]{0:T(1024)S(1)} %pad_clamp_fusion), kind=kCustom, calls=%fused_computation.1 | custom fusion | bytes 24600 | tf_op jit(solution)/shard_map/gather | solution.py:87
  35.5 1.7 %gather_fusion = bf16[6,4,1024]{2,1,0:T(4,128)(2,1)S(1)} fusion(bf16[91,4,1024]{2,1,0:T(4,128)(2,1)} %param.14, s32[1024]{0:T(1024)S(1)} %pad_clamp_fusion), kind=kCustom, calls=%fused_computation | custom fusion | bytes 98328 | tf_op jit(solution)/shard_map/gather | solution.py:85
  37.2 1.8 %bitcast_reduce_fusion = (f32[6,256]{1,0:T(8,128)S(1)}, f32[6,1024,256]{1,2,0:T(8,128)S(1)}) fusion(f32[6,1024]{1,0:T(8,128)S(1)} %convert_element_type.41, bf16[6,4,1024]{2,1,0:T(4,128)(2,1)S(1)} %gather_fusion, bf16[1,6,4,256]{3,2,1,0:T(4,128)(2,1)} %param.11), kind=kOutput, calls=%fused_computation.4 | convolution fusion | flops 15727104 | bytes 6383616 | tf_op jit(solution)/shard_map/skp,skd->spd/dot_general | solution.py:86
  39.1 1.0 multiply_reduce_fusion.1
  40.1 2.5 %add_convert_fusion = bf16[6,256,1024]{2,1,0:T(8,128)(2,1)} fusion(f32[6,1024,256]{1,2,0:T(8,128)S(1)} %get-tuple-element.8, f32[1024]{0:T(1024)S(1)} %copy-done.2, f32[1024]{0:T(1024)S(1)} %copy-done.3, f32[6,256]{1,0:T(8,128)S(1)} %add_rsqrt_fusion, f32[6,256]{1,0:T(8,128)S(1)} %broadcast_multiply_fusion, f32[6,1024]{1,0:T(8,128)S(1)} %convert_element_type.41), kind=kLoop, calls=%fused_computation.5 | loop fusion | flops 9437184 | bytes 9482240 | tf_op jit(solution)/shard_map/convert_element_type | solution.py:90
  43.8 0.8 reduce.2
  45.0 4.4 %convolution_multiply_fusion = f32[1536,16]{0,1:T(8,128)S(1)} fusion(bf16[1536,1024]{1,0:T(8,128)(2,1)} %bitcast.56, f32[1024,16]{0,1:T(8,128)S(1)} %reshape.77), kind=kOutput, calls=%fused_computation.8 | convolution fusion | flops 302014464 | bytes 3309568 | tf_op jit(solution)/shard_map/dot_general | solution.py:102
  49.6 22.6 %all_to_all.15 = f32[16,256,16]{1,2,0:T(8,128)S(1)} all-to-all(f32[16,256,16]{1,2,0:T(8,128)S(1)} %broadcast_in_dim.34), channel_id=1, replica_groups=mesh['dp_0'=4,'dp_1'=8,'var'=16] {'var'}, dimensions={0} | all-to-all | bytes 524288 | tf_op jit(solution)/shard_map/all_to_all | solution.py:20
  72.5 2.0 %copy.22 = bf16[4,8,32,1024]{3,2,1,0:T(8,128)(2,1)S(1)} copy(bf16[4,8,32,1024]{3,2,0,1:T(8,128)(2,1)} %bitcast.58) | data formatting | bytes 4194304 | tf_op jit(solution)/shard_map/transpose | solution.py:33
  75.1 4.7 %convolution_convert_fusion = bf16[1536,1024]{1,0:T(8,128)(2,1)} fusion(bf16[1536,1024]{1,0:T(8,128)(2,1)S(1)} %bitcast.57, bf16[1024,1024]{1,0:T(8,128)(2,1)S(1)} %bitcast.59), kind=kOutput, calls=%fused_computation.7 | convolution fusion | flops 3222798336 | bytes 8388608 | tf_op jit(solution)/shard_map/dot_general | solution.py:99
  79.8 4.7 %copy.23 = bf16[1536,1024]{0,1:T(8,128)(2,1)} copy(bf16[1536,1024]{1,0:T(8,128)(2,1)} %convolution_convert_fusion) | data formatting | bytes 6291456 | tf_op jit(solution)/shard_map/convert_element_type | solution.py:107
  84.5 7.5 %reshape_reshape.7 = bf16[6,256,16,64]{1,0,3,2:T(8,128)(2,1)} reshape(bf16[1536,1024]{0,1:T(8,128)(2,1)} %copy.23) | data formatting | bytes 6291456 | tf_op jit(solution)/shard_map/reshape;reshape | solution.py:113
  92.0 5.9 %multiply_reduce_fusion = bf16[256,16,64]{0,2,1:T(8,128)(2,1)} fusion(f32[256,16,6]{0,2,1:T(8,128)S(1)} %get-tuple-element.5, bf16[6,256,16,64]{1,0,3,2:T(8,128)(2,1)} %reshape_reshape.7), kind=kLoop, calls=%fused_computation.2 | loop fusion | flops 4456448 | bytes 3768320
  97.8 2.0 %copy.35 = bf16[256,16,64]{2,1,0:T(8,128)(2,1)S(1)} copy(bf16[256,16,64]{0,2,1:T(8,128)(2,1)} %multiply_reduce_fusion) | data formatting | bytes 1048576 | tf_op jit(solution)/shard_map/sph,sphe->phe/dot_general | solution.py:110
  99.8 1.5 %convert_element_type.46 = bf16[16,16,1024]{2,1,0:T(8,128)(2,1)} reshape(bf16[256,16,64]{2,1,0:T(8,128)(2,1)S(1)} %copy.35) | data formatting | bytes 1048576 | tf_op jit(solution)/shard_map/convert_element_type | solution.py:118
  101.3 1.1 pad_maximum_fusion
  102.4 23.6 %all_to_all.16 = bf16[16,16,1040]{2,1,0:T(8,128)(2,1)S(1)} all-to-all(bf16[16,16,1040]{2,1,0:T(8,128)(2,1)S(1)} %pad_maximum_fusion), channel_id=1, replica_groups=mesh['dp_0'=4,'dp_1'=8,'var'=16] {'var'}, dimensions={0} | all-to-all | bytes 1064960 | tf_op jit(solution)/shard_map/all_to_all | solution.py:53
  126.4 1.0 fusion
  (32 shorter events, 2.3 us)
Async XLA Ops:
  6.5 119.8 %copy-start = (bf16[1024,1024]{1,0:T(8,128)(2,1)S(1)}, bf16[1024,1024]{1,0:T(8,128)(2,1)}, u32[]{:S(2)}) copy-start(bf16[1024,1024]{1,0:T(8,128)(2,1)} %param.21) | copy-start | bytes 6291460
  6.5 66.0 %all-gather.4.cloned.1.call-start = ((), (), s32[]{:S(2)}) async-start(), calls=%async_computation.3 | async-start | bytes 2359296 | tf_op jit(solution)/shard_map/all_gather | solution.py:30
  22.3 21.0 %all-to-all-start = ((f32[32,1,512]{2,1,0:T(1,128)}), f32[32,1,512]{2,1,0:T(1,128)S(1)}, u32[]{:S(2)}, u32[]{:S(2)}) async-start(f32[32,1,512]{2,1,0:T(1,128)} %reshape.101), calls=%async_computation | async-start | bytes 131072 | tf_op jit(solution)/shard_map/all_to_all | solution.py:20
  39.1 1.1 copy-start.2
  39.1 1.1 copy-start.3
  72.5 2.5 %copy-start.1 = (bf16[6,256,1024]{2,1,0:T(8,128)(2,1)S(1)}, bf16[6,256,1024]{2,1,0:T(8,128)(2,1)}, u32[]{:S(2)}) copy-start(bf16[6,256,1024]{2,1,0:T(8,128)(2,1)} %add_convert_fusion) | copy-start | bytes 9437188
Sparse Core Ops, SparseCore 0:
  19.6 46.1 all-gather.3
where the time goes:
time: 135 us; the launch traced here: 134 us
  blocking collectives  59.1 us (44%)
  local copies, waits for them, and re-layouts  24.5 us (18%)
  between operations  14.3 us (11%)
  matrix products  13 us (10%)
  other arithmetic  12.3 us (9%)
  starting transfers between devices  11 us (8%)
    all_to_all x1, blocking collectives, sum_at_owner(): pieces = lax.all_to_all(cut_along(x, dim, length), axis, 0, 0, tiled=True)  23.6 us
    all_to_all x1, blocking collectives, sent_to_all(): return lax.all_to_all(copies, axis, split_axis=0, concat_axis=0, tiled=True)  22.6 us
    all_gather x1, blocking collectives, gather_in_order(): pieces = lax.all_gather(pieces, axes[k])  12.9 us
    all_to_all x1, starting transfers between devices, sent_to_all(): return lax.all_to_all(copies, axis, split_axis=0, concat_axis=0, tiled=True)  11 us
    another operation x1, local copies, waits for them, and re-layouts, on_device(): values.reshape(slots, patches, heads, head_size)  7.51 us
    unnamed x2, other arithmetic  5.99 us
    dot_general x1, matrix products, on_device(): jnp.dot(flat, gathered_by_axis(value_weight, DP, (0, 1), 0), preferred_el...  4.74 us
    convert_element_type x1, local copies, waits for them, and re-layouts, on_device(): values = values.astype(jnp.bfloat16).reshape(slots, patches, width)  4.66 us
  transfers between devices with their start and end apart: 2, of which 0 were waited for; matrix products, arithmetic and copies ran while one was open for 14% of the time, Pallas kernels for 0%

commit v1 on v0

v1 whole, which is shorter than its diff:
```python
import math

import jax
import jax.numpy as jnp
from jax import lax
from jax.experimental import pallas as pl
from jax.experimental.pallas import tpu as pltpu
from jax.sharding import Mesh
from jax.sharding import PartitionSpec as P

DP = ("dp_0", "dp_1")
F32 = jnp.float32
BF16 = jnp.bfloat16
PAIRS = [(k, l) for k in range(5) for l in range(k, 5)]


def whole(memory_space=pltpu.VMEM):
    return pl.BlockSpec(memory_space=memory_space)


def iota(shape, dim):
    return lax.broadcasted_iota(jnp.int32, shape, dim)


def head_slice_kernel(var_ref, wk_ref, wv_ref, out_ref):
    head = var_ref[0]
    at = pl.multiple_of((head // 2) * 128, 128)
    half = head % 2
    wk = wk_ref[:, pl.ds(at, 128)].astype(F32)
    wv = wv_ref[:, pl.ds(at, 128)].astype(F32)
    lane = iota(wk.shape, 1)
    both = jnp.where(lane // 64 == half, wv, pltpu.roll(wk, 64, 1)).astype(BF16)
    for d in range(out_ref.shape[0]):
        out_ref[d] = both


def table_kernel(ids_ref, pix_ref, pw_ref, ve_ref, gain_ref, bias_ref, hi_ref, lo_ref, send_ref, ac, af, rows, chunk):
    n_pw, width = pw_ref.shape
    n_ve = ve_ref.shape[0]
    total = af.shape[0]
    at = n_pw + 4
    gain = gain_ref[...]

    def centered(x):
        return x - jnp.mean(x, axis=-1, keepdims=True)

    pw = centered(pw_ref[...].astype(F32))
    ac[0:n_pw, :] = pw
    af[0:n_pw, :] = pw * gain
    af[n_pw:at, :] = jnp.zeros((at - n_pw, width), F32)
    ve = centered(ve_ref[...].astype(F32))
    ac[at : at + n_ve, :] = ve
    af[at : at + n_ve, :] = ve * gain
    af[at + n_ve : at + n_ve + 1, :] = bias_ref[...]
    af[at + n_ve + 1 : total, :] = jnp.zeros((total - at - n_ve - 1, width), F32)
    a = af[...]
    hi = a.astype(BF16)
    hi_ref[...] = hi
    lo_ref[...] = (a - hi.astype(F32)).astype(BF16)

    slots = ids_ref.shape[1]
    rows[...] = jnp.zeros(rows.shape, F32)
    sub = iota((8, 256), 0)
    lane = iota((8, 256), 1)
    meta = jnp.zeros((8, 256), F32)
    for s in range(slots):
        v = ids_ref[0, s]
        for k in range(4):
            rows[k, s : s + 1, :] = ac[pl.ds(4 * v + k, 1), :]
        rows[4, s : s + 1, :] = ac[pl.ds(at + v, 1), :]
        meta = jnp.where((sub == s) & (lane == 48), v.astype(F32), meta)
    for i, (k, l) in enumerate(PAIRS):
        g = jnp.sum(rows[k] * rows[l], axis=-1, keepdims=True) * ((1.0 if k == l else 2.0) / width)
        for part in range(3):
            top = g.astype(BF16).astype(F32)
            meta = jnp.where(lane == 16 * part + i, top, meta)
            g = g - top
    chunk[0 : 4 * slots, :] = pix_ref[...].astype(F32)
    chunk[4 * slots :, :] = meta
    packed = chunk[...].astype(BF16)
    for j in range(send_ref.shape[0]):
        send_ref[j] = packed


def project_kernel(hi_ref, lo_ref, w_ref, thi_ref, tlo_ref):
    w = w_ref[...]
    t = jnp.dot(hi_ref[...], w, preferred_element_type=F32)
    t = t + jnp.dot(lo_ref[...], w, preferred_element_type=F32)
    hi = t.astype(BF16)
    thi_ref[...] = hi
    tlo_ref[...] = (t - hi.astype(F32)).astype(BF16)


def attend_kernel(var_ref, count_ref, x_ref, thi_ref, tlo_ref, query_ref, out_ref, w_scr, v_scr):
    head = var_ref[0]
    count = count_ref[0]
    half = head % 2
    slots = w_scr.shape[0] // 5
    entries = thi_ref.shape[0]
    n_pw = 364
    at = n_pw + 4
    x = x_ref[...]
    n_rows = x.shape[0]

    n = iota((slots, n_rows), 0)
    group = (n * 43) >> 8
    base = group * 32
    within = n - group * 6
    col = iota((slots, n_rows), 1)

    def picked(target):
        p = jnp.where(col == target, 1.0, 0.0).astype(BF16)
        return p

    meta = jnp.dot(picked(base + 24 + within), x[:, :128], preferred_element_type=F32)
    c = [jnp.dot(picked(base + within * 4 + k), x, preferred_element_type=F32) for k in range(4)]
    gram = meta + pltpu.roll(meta, 112, 1) + pltpu.roll(meta, 96, 1)
    ids = meta[:, 48:49].astype(jnp.int32)

    col = iota((slots, entries), 1)
    lane = iota((slots, 128), 1)
    is_value = lane // 64 == half
    q = query_ref[pl.ds(head, 1), :] * (1.0 / math.sqrt(query_ref.shape[1]))
    q2 = jnp.concatenate([q, q], axis=1)
    thi, tlo = thi_ref[...], tlo_ref[...]
    keyed = []
    for k in range(5):
        target = 4 * ids + k if k < 4 else at + ids
        pick = jnp.where(col == target, 1.0, 0.0).astype(BF16)
        thi_k = jnp.dot(pick, thi, preferred_element_type=F32)
        t_k = thi_k + jnp.dot(pick, tlo, preferred_element_type=F32)
        keyed.append(jnp.sum(jnp.where(is_value, 0.0, t_k * q2), axis=1, keepdims=True))
        v_scr[k * slots : (k + 1) * slots, :] = jnp.where(is_value, t_k, 0.0).astype(BF16)
    last = entries - 16
    tail = thi[last:, :].astype(F32) + tlo[last:, :].astype(F32)
    bias_row = tail[at + 91 - last : at + 92 - last, :]
    is_value_row = is_value[0:1, :]
    key_bias = jnp.sum(jnp.where(is_value_row, 0.0, bias_row * q2), axis=1, keepdims=True)
    value_bias = jnp.where(is_value_row, bias_row, 0.0)

    def g(k, l):
        i = PAIRS.index((k, l))
        return gram[:, i : i + 1]

    spread = g(4, 4)
    for k in range(4):
        inner = g(k, 4)
        for l in range(k, 4):
            inner = inner + g(k, l) * c[l]
        spread = spread + c[k] * inner
    r = lax.rsqrt(jnp.maximum(spread, 0.0) + 1e-05)
    dots = keyed[4]
    for k in range(4):
        dots = dots + c[k] * keyed[k]
    scores = r * dots + key_bias
    scores = jnp.where(iota(scores.shape, 0) < count, scores, -1e30)
    peak = jnp.max(scores, axis=0, keepdims=True)
    expo = jnp.exp(scores - peak)
    share = expo * (1.0 / jnp.sum(expo, axis=0, keepdims=True)) * r
    for k in range(4):
        w_scr[k * slots : (k + 1) * slots, :] = (share * c[k]).astype(BF16)
    w_scr[4 * slots :, :] = share.astype(BF16)
    mixed = lax.dot_general(
        w_scr[...], v_scr[...], (((0,), (0,)), ((), ())), preferred_element_type=F32
    )
    out_ref[...] = (mixed + value_bias).astype(BF16)


def project_out_kernel(m_ref, wo_ref, out_ref):
    parts = [m_ref[2 * i].astype(F32) + m_ref[2 * i + 1].astype(F32) for i in range(m_ref.shape[0] // 2)]
    mixed = jnp.concatenate(parts, axis=1).astype(BF16)
    out_ref[...] = jnp.dot(mixed, wo_ref[...], preferred_element_type=F32).astype(BF16)


def cost(flops, moved):
    return pl.CostEstimate(flops=flops, transcendentals=0, bytes_accessed=moved)


def on_device(
    pixels,
    var_ids,
    counts,
    patch_weight,
    var_embed,
    norm_gain,
    norm_bias,
    key_weight,
    value_weight,
    query,
    out_weight,
):
    slots, pp, patches = pixels.shape[1:]
    n_var, width = var_embed.shape
    n_dp = lax.axis_size(DP)
    n_sv = lax.axis_size("var")
    all_slots = slots * n_sv
    entries = 464
    smem, vmem = whole(pltpu.SMEM), whole()
    var = lax.axis_index("var").astype(jnp.int32).reshape(1)

    slices = pl.pallas_call(
        head_slice_kernel,
        out_shape=jax.ShapeDtypeStruct((n_dp, key_weight.shape[0], 128), BF16),
        in_specs=[smem, vmem, vmem],
        out_specs=vmem,
        name="head_slice",
    )(var, key_weight, value_weight)
    weights = lax.all_to_all(slices, DP, 0, 0, tiled=True)

    hi, lo, send = pl.pallas_call(
        table_kernel,
        out_shape=(
            jax.ShapeDtypeStruct((entries, width), BF16),
            jax.ShapeDtypeStruct((entries, width), BF16),
            jax.ShapeDtypeStruct((n_sv, 32, patches), BF16),
        ),
        in_specs=[smem] + [vmem] * 5,
        out_specs=(vmem, vmem, vmem),
        scratch_shapes=[
            pltpu.VMEM((entries, width), F32),
            pltpu.VMEM((entries, width), F32),
            pltpu.VMEM((5, 8, width), F32),
            pltpu.VMEM((32, patches), F32),
        ],
        cost_estimate=cost(20 * entries * width, 8 * entries * width),
        compiler_params=pltpu.CompilerParams(vmem_limit_bytes=24 << 20),
        name="tables",
    )(
        var_ids,
        pixels.reshape(slots * pp, patches),
        patch_weight.reshape(n_var * pp, width),
        var_embed,
        norm_gain.reshape(1, width),
        norm_bias.reshape(1, width),
    )
    weights, send = lax.optimization_barrier((weights, send))
    gathered = lax.all_to_all(send, "var", 0, 0, tiled=True)

    thi, tlo = pl.pallas_call(
        project_kernel,
        out_shape=(jax.ShapeDtypeStruct((entries, 128), BF16),) * 2,
        in_specs=[vmem] * 3,
        out_specs=(vmem, vmem),
        cost_estimate=cost(4 * entries * width * 128, 5 * entries * width),
        compiler_params=pltpu.CompilerParams(vmem_limit_bytes=16 << 20),
        name="project",
    )(hi, lo, weights.reshape(width, 128))

    mixed = pl.pallas_call(
        attend_kernel,
        out_shape=jax.ShapeDtypeStruct((patches, 128), BF16),
        in_specs=[smem, smem, vmem, vmem, vmem, vmem],
        out_specs=vmem,
        scratch_shapes=[
            pltpu.VMEM((5 * all_slots, patches), BF16),
            pltpu.VMEM((5 * all_slots, 128), BF16),
        ],
        compiler_params=pltpu.CompilerParams(vmem_limit_bytes=24 << 20),
        name="attend",
    )(var, counts, gathered.reshape(n_sv * 32, patches), thi, tlo, query)
    owned = lax.all_to_all(mixed.reshape(n_sv, patches // n_sv, 128), "var", 0, 0, tiled=True)

    out = pl.pallas_call(
        project_out_kernel,
        out_shape=jax.ShapeDtypeStruct((patches // n_sv, width), BF16),
        in_specs=[vmem, vmem],
        out_specs=vmem,
        compiler_params=pltpu.CompilerParams(vmem_limit_bytes=16 << 20),
        name="project_out",
    )(owned, out_weight)
    return out[None]


def solution(mesh):
    torus = Mesh(mesh.devices.reshape(4, 8, mesh.shape["var"]), ("dp_0", "dp_1", "var"))
    return jax.shard_map(
        on_device,
        mesh=torus,
        in_specs=(
            P(DP, "var", None, None),
            P(DP, "var"),
            P(DP),
            P(),
            P(),
            P(),
            P(),
            P(DP, None),
            P(DP, None),
            P(),
            P(),
        ),
        out_specs=P(DP, "var", None),
        check_vma=False,
    )
```

time: 135 us -> 60.8 us (0.45)
  blocking collectives: 59.1 us -> 10.5 us
  local copies, waits for them, and re-layouts: 24.5 us -> 5.88 us
  starting transfers between devices: 11 us -> 24.6 us
  between operations: 14.3 us -> 0.78 us
  matrix products: 13 us -> 0 us
  other arithmetic: 12.3 us -> 0 us
  waiting for transfers between devices: 0.04 us -> 12.1 us
  Pallas kernels: 0 us -> 6.58 us
    all_to_all x2 -> x1, blocking collectives: 46.2 us -> 10.5 us  [on_device(): lax.all_to_all(mixed.reshape(n_sv, patches // n_sv, 128), 'var', 0, 0, ti...]
    all_to_all x1 -> x2, starting transfers between devices: 11 us -> 24.6 us  [the longest x1 13.7 us: on_device(): weights = lax.all_to_all(slices, DP, 0, 0, tiled=True)]
    dot_general x5 -> x0, matrix products: 13 us -> none  [the longest x1 4.74 us: on_device(): jnp.dot(flat, gathered_by_axis(value_weight, DP, (0, 1), 0), preferred_el...]
    all_gather x1 -> x0, blocking collectives: 12.9 us -> none  [gather_in_order(): pieces = lax.all_gather(pieces, axes[k])]
    all_to_all x1 -> x2, waiting for transfers between devices: 0.01 us -> 12.1 us  [the longest x1 8.01 us: on_device(): gathered = lax.all_to_all(send, 'var', 0, 0, tiled=True)]
    another operation x1 -> x0, local copies, waits for them, and re-layouts: 7.51 us -> none  [on_device(): values.reshape(slots, patches, heads, head_size)]
    pallas_call x0 -> x5, Pallas kernels: none -> 6.58 us  [the longest x1 1.99 us: on_device(): pl.pallas_call(table_kernel, out_shape=(jax.ShapeDtypeStruct((entries, wi...]
    convert_element_type x3 -> x0, local copies, waits for them, and re-layouts: 6.29 us -> none  [the longest x1 4.66 us: on_device(): values = values.astype(jnp.bfloat16).reshape(slots, patches, width)]
  transfers between devices with their start and end apart: 2 -> 2, of which waited for: 0 -> 2; matrix products, arithmetic and copies ran while one was open for 14% -> 3% of each run, Pallas kernels for 0% -> 4%
where the time goes in v1:
time: 60.8 us; the launch traced here: 60.4 us
  starting transfers between devices  24.6 us (40%)
  waiting for transfers between devices  12.1 us (20%)
  blocking collectives  10.5 us (17%)
  Pallas kernels  6.58 us (11%)
  local copies, waits for them, and re-layouts  5.88 us (10%)
  between operations  0.78 us (1%)
    all_to_all x1, starting transfers between devices, on_device(): weights = lax.all_to_all(slices, DP, 0, 0, tiled=True)  13.7 us
    all_to_all x1, starting transfers between devices, on_device(): gathered = lax.all_to_all(send, 'var', 0, 0, tiled=True)  10.8 us
    all_to_all x1, blocking collectives, on_device(): lax.all_to_all(mixed.reshape(n_sv, patches // n_sv, 128), 'var', 0, 0, ti...  10.5 us
    all_to_all x1, waiting for transfers between devices, on_device(): gathered = lax.all_to_all(send, 'var', 0, 0, tiled=True)  8.01 us
    unnamed x22, local copies, waits for them, and re-layouts  4.33 us
    all_to_all x1, waiting for transfers between devices, on_device(): weights = lax.all_to_all(slices, DP, 0, 0, tiled=True)  4.13 us
    pallas_call x1, Pallas kernels, on_device(): pl.pallas_call(table_kernel, out_shape=(jax.ShapeDtypeStruct((entries, wi...  1.99 us
    pallas_call x1, Pallas kernels, on_device(): pl.pallas_call(head_slice_kernel, out_shape=jax.ShapeDtypeStruct((n_dp, k...  1.73 us
  transfers between devices with their start and end apart: 2, of which 2 were waited for; matrix products, arithmetic and copies ran while one was open for 3% of the time, Pallas kernels for 4%

profile of v1, /device:TPU:1, one launch (start us, length us, event | category | flops | bytes accessed | tf_op | source)
XLA Modules:
  0.0 60.4 jit_solution(15426681499652842801)
XLA Ops:
  0.0 0.0 copy-start.9
  0.0 0.0 copy-start.5
  0.0 1.7 %head_slice.1 = bf16[32,32,128]{2,1,0:T(8,128)(2,1)} custom-call(s32[1]{0:T(128)} %bitcast.var_ref, bf16[32,1024]{1,0:T(8,128)(2,1)} %wk_ref.1, bf16[32,1024]{1,0:T(8,128)(2,1)} %wv_ref.1), custom_call_target="tpu_custom_call" | custom-call | tf_op jit(solution)/shard_map/head_slice/pallas_call | solution.py:201
  1.8 13.7 %all-to-all-start = ((bf16[32,32,128]{2,1,0:T(8,128)(2,1)}), bf16[32,32,128]{2,1,0:T(8,128)(2,1)S(1)}, u32[]{:S(2)}, u32[]{:S(2)}) async-start(bf16[32,32,128]{2,1,0:T(8,128)(2,1)} %head_slice.1), calls=%async_computation | async-start | bytes 524288 | tf_op jit(solution)/shard_map/all_to_all | solution.py:208
  15.5 1.5 %reshape.26.pw_ref = bf16[364,1024]{1,0:T(8,128)(2,1)S(1)} reshape(bf16[91,4,1024]{2,1,0:T(4,128)(2,1)} %param.14) | data formatting | bytes 1490944 | tf_op jit(solution)/shard_map/reshape | solution.py:231
  17.0 0.0 copy-done.10
  17.0 0.0 copy-start.6
  17.1 0.0 copy-done.7
  17.1 0.0 copy-done.8
  17.1 0.0 copy-done.9
  17.1 0.0 copy-start
  17.1 2.0 %tables.1 = (bf16[464,1024]{1,0:T(8,128)(2,1)S(1)}, bf16[464,1024]{1,0:T(8,128)(2,1)S(1)}, bf16[16,32,256]{2,1,0:T(8,128)(2,1)}) custom-call(s32[1,6]{1,0:T(1,128)S(1)} %copy-done.9, bf16[24,256]{1,0:T(8,128)(2,1)S(1)} %reshape.25.pix_ref, bf16[364,1024]{1,0:T(8,128)(2,1)S(1)} %reshape.26.pw_ref, bf16[91,1024]{1,0:T(8,128)(2,1)S(1)} %copy-done.5, ...), custom_call_target="tpu_custom_call" | custom-call | flops 9502720 | bytes 3801088 | tf_op jit(solution)/shard_map/tables/pallas_call | solution.py:210
  19.1 0.9 %copy-done.1 = bf16[464,1024]{1,0:T(8,128)(2,1)} copy-done((bf16[464,1024]{1,0:T(8,128)(2,1)}, bf16[464,1024]{1,0:T(8,128)(2,1)S(1)}, u32[]{:S(2)}) %copy-start.1) | copy-done | bytes 950296
  20.1 1.0 %copy-done.3 = bf16[464,1024]{1,0:T(8,128)(2,1)} copy-done((bf16[464,1024]{1,0:T(8,128)(2,1)}, bf16[464,1024]{1,0:T(8,128)(2,1)S(1)}, u32[]{:S(2)}) %copy-start.3) | copy-done | bytes 950296
  21.0 4.1 %all-to-all-done = bf16[32,32,128]{2,1,0:T(8,128)(2,1)S(1)} async-done(((bf16[32,32,128]{2,1,0:T(8,128)(2,1)}), bf16[32,32,128]{2,1,0:T(8,128)(2,1)S(1)}, u32[]{:S(2)}, u32[]{:S(2)}) %all-to-all-start) | async-done | bytes 262176 | tf_op jit(solution)/shard_map/all_to_all | solution.py:208
  25.2 10.8 %all-to-all-start.1 = ((bf16[16,32,256]{2,1,0:T(8,128)(2,1)}), bf16[16,32,256]{2,1,0:T(8,128)(2,1)S(1)}, u32[]{:S(2)}, u32[]{:S(2)}) async-start(bf16[16,32,256]{2,1,0:T(8,128)(2,1)} %get-tuple-element.13), calls=%async_computation.1 | async-start | bytes 524288 | tf_op jit(solution)/shard_map/all_to_all | solution.py:237
  36.7 1.2 %copy-done.2 = bf16[464,1024]{1,0:T(8,128)(2,1)S(1)} copy-done((bf16[464,1024]{1,0:T(8,128)(2,1)S(1)}, bf16[464,1024]{1,0:T(8,128)(2,1)}, u32[]{:S(2)}) %copy-start.2) | copy-done | bytes 950296
  37.9 1.2 %copy-done.4 = bf16[464,1024]{1,0:T(8,128)(2,1)S(1)} copy-done((bf16[464,1024]{1,0:T(8,128)(2,1)S(1)}, bf16[464,1024]{1,0:T(8,128)(2,1)}, u32[]{:S(2)}) %copy-start.4) | copy-done | bytes 950296
  39.0 0.7 %project.1 = (bf16[464,128]{1,0:T(8,128)(2,1)S(1)}, bf16[464,128]{1,0:T(8,128)(2,1)S(1)}) custom-call(bf16[464,1024]{1,0:T(8,128)(2,1)S(1)} %copy-done.2, bf16[464,1024]{1,0:T(8,128)(2,1)S(1)} %copy-done.4, bf16[1024,128]{1,0:T(8,128)(2,1)S(1)} %bitcast.7), custom_call_target="tpu_custom_call" | custom-call | flops 243269632 | bytes 2375680 | tf_op jit(solution)/shard_map/project/pallas_call | solution.py:239
  39.7 8.0 %all-to-all-done.1 = bf16[16,32,256]{2,1,0:T(8,128)(2,1)S(1)} async-done(((bf16[16,32,256]{2,1,0:T(8,128)(2,1)}), bf16[16,32,256]{2,1,0:T(8,128)(2,1)S(1)}, u32[]{:S(2)}, u32[]{:S(2)}) %all-to-all-start.1) | async-done | bytes 262176 | tf_op jit(solution)/shard_map/all_to_all | solution.py:237
  47.7 1.2 %attend.1 = bf16[256,128]{1,0:T(8,128)(2,1)S(1)} custom-call(s32[1]{0:T(128)} %bitcast.var_ref, s32[1]{0:T(128)S(6)} %copy.12.count_ref, bf16[512,256]{1,0:T(8,128)(2,1)S(1)} %bitcast.8, bf16[464,128]{1,0:T(8,128)(2,1)S(1)} %get-tuple-element.17.thi_ref, bf16[464,128]{1,0:T(8,128)(2,1)S(1)} %get-tuple-element.18.tlo_ref, f32[16,64]{1,0:T(8,128)S(1)} %copy-done.6), custom_call_target="tpu_custom_call" | custom-call | tf_op jit(solution)/shard_map/attend/pallas_call | solution.py:249
  48.9 10.5 %all_to_all.15.m_ref = bf16[16,16,128]{2,1,0:T(8,128)(2,1)S(1)} all-to-all(bf16[16,16,128]{2,1,0:T(8,128)(2,1)S(1)} %bitcast.9), channel_id=1, replica_groups=mesh['dp_0'=4,'dp_1'=8,'var'=16] {'var'}, dimensions={0} | all-to-all | bytes 131072 | tf_op jit(solution)/shard_map/all_to_all | solution.py:261
  59.4 0.0 copy-done
  59.4 1.0 %project_out.1 = bf16[16,1024]{1,0:T(8,128)(2,1)} custom-call(bf16[16,16,128]{2,1,0:T(8,128)(2,1)S(1)} %all_to_all.15.m_ref, bf16[1024,1024]{1,0:T(8,128)(2,1)S(1)} %copy-done), custom_call_target="tpu_custom_call" | custom-call | tf_op jit(solution)/shard_map/project_out/pallas_call | solution.py:263
  (10 shorter events, 0.0 us)
Async XLA Ops:
  0.0 17.0 %copy-start.10 = (bf16[1,6,4,256]{3,2,1,0:T(4,128)(2,1)S(1)}, bf16[1,6,4,256]{3,2,1,0:T(4,128)(2,1)}, u32[]{:S(2)}) copy-start(bf16[1,6,4,256]{3,2,1,0:T(4,128)(2,1)} %param.11) | copy-start | bytes 36868
  0.0 17.1 %copy-start.7 = (f32[1024]{0:T(1024)S(1)}, f32[1024]{0:T(1024)}, u32[]{:S(2)}) copy-start(f32[1024]{0:T(1024)} %param.16) | copy-start | bytes 12292
  0.0 17.1 %copy-start.8 = (f32[1024]{0:T(1024)S(1)}, f32[1024]{0:T(1024)}, u32[]{:S(2)}) copy-start(f32[1024]{0:T(1024)} %param.17) | copy-start | bytes 12292
  0.0 17.1 %copy-start.9 = (s32[1,6]{1,0:T(1,128)S(1)}, s32[1,6]{1,0:T(1,128)}, u32[]{:S(2)}) copy-start(s32[1,6]{1,0:T(1,128)} %ids_ref.1) | copy-start | bytes 76
  0.0 17.1 %copy-start.5 = (bf16[91,1024]{1,0:T(8,128)(2,1)S(1)}, bf16[91,1024]{1,0:T(8,128)(2,1)}, u32[]{:S(2)}) copy-start(bf16[91,1024]{1,0:T(8,128)(2,1)} %ve_ref.1) | copy-start | bytes 559108
  1.8 23.4 %all-to-all-start = ((bf16[32,32,128]{2,1,0:T(8,128)(2,1)}), bf16[32,32,128]{2,1,0:T(8,128)(2,1)S(1)}, u32[]{:S(2)}, u32[]{:S(2)}) async-start(bf16[32,32,128]{2,1,0:T(8,128)(2,1)} %head_slice.1), calls=%async_computation | async-start | bytes 524288 | tf_op jit(solution)/shard_map/all_to_all | solution.py:208
  17.0 30.7 %copy-start.6 = (f32[16,64]{1,0:T(8,128)S(1)}, f32[16,64]{1,0:T(8,128)}, u32[]{:S(2)}) copy-start(f32[16,64]{1,0:T(8,128)} %query_ref.1) | copy-start | bytes 12292
  17.1 42.3 %copy-start = (bf16[1024,1024]{1,0:T(8,128)(2,1)S(1)}, bf16[1024,1024]{1,0:T(8,128)(2,1)}, u32[]{:S(2)}) copy-start(bf16[1024,1024]{1,0:T(8,128)(2,1)} %wo_ref.1) | copy-start | bytes 6291460
  19.1 0.9 %copy-start.1 = (bf16[464,1024]{1,0:T(8,128)(2,1)}, bf16[464,1024]{1,0:T(8,128)(2,1)S(1)}, u32[]{:S(2)}) copy-start(bf16[464,1024]{1,0:T(8,128)(2,1)S(1)} %get-tuple-element.14.hi_ref) | copy-start | bytes 2850820
  20.1 1.0 %copy-start.3 = (bf16[464,1024]{1,0:T(8,128)(2,1)}, bf16[464,1024]{1,0:T(8,128)(2,1)S(1)}, u32[]{:S(2)}) copy-start(bf16[464,1024]{1,0:T(8,128)(2,1)S(1)} %get-tuple-element.15.lo_ref) | copy-start | bytes 2850820
  25.2 22.5 %all-to-all-start.1 = ((bf16[16,32,256]{2,1,0:T(8,128)(2,1)}), bf16[16,32,256]{2,1,0:T(8,128)(2,1)S(1)}, u32[]{:S(2)}, u32[]{:S(2)}) async-start(bf16[16,32,256]{2,1,0:T(8,128)(2,1)} %get-tuple-element.13), calls=%async_computation.1 | async-start | bytes 524288 | tf_op jit(solution)/shard_map/all_to_all | solution.py:237
  36.7 1.2 %copy-start.2 = (bf16[464,1024]{1,0:T(8,128)(2,1)S(1)}, bf16[464,1024]{1,0:T(8,128)(2,1)}, u32[]{:S(2)}) copy-start(bf16[464,1024]{1,0:T(8,128)(2,1)} %copy-done.1) | copy-start | bytes 2850820
  37.9 1.2 %copy-start.4 = (bf16[464,1024]{1,0:T(8,128)(2,1)S(1)}, bf16[464,1024]{1,0:T(8,128)(2,1)}, u32[]{:S(2)}) copy-start(bf16[464,1024]{1,0:T(8,128)(2,1)} %copy-done.3) | copy-start | bytes 2850820

commit v2 on v1

--- a/solution.py
+++ b/solution.py
@@ -1,5 +1,3 @@
-import math
-
 import jax
 import jax.numpy as jnp
 from jax import lax
@@ -9,6 +7,7 @@
 from jax.sharding import PartitionSpec as P
 
 DP = ("dp_0", "dp_1")
+VAR = ("y", "core")
 F32 = jnp.float32
 BF16 = jnp.bfloat16
 PAIRS = [(k, l) for k in range(5) for l in range(k, 5)]
@@ -22,14 +21,28 @@
     return lax.broadcasted_iota(jnp.int32, shape, dim)
 
 
-def head_slice_kernel(var_ref, wk_ref, wv_ref, out_ref):
-    head = var_ref[0]
-    at = pl.multiple_of((head // 2) * 128, 128)
-    half = head % 2
-    wk = wk_ref[:, pl.ds(at, 128)].astype(F32)
-    wv = wv_ref[:, pl.ds(at, 128)].astype(F32)
-    lane = iota(wk.shape, 1)
-    both = jnp.where(lane // 64 == half, wv, pltpu.roll(wk, 64, 1)).astype(BF16)
+def split3(x):
+    top = x.astype(BF16).astype(F32)
+    mid = (x - top).astype(BF16).astype(F32)
+    return top, mid, (x - top - mid).astype(BF16).astype(F32)
+
+
+def head_slice_kernel(chip_ref, wk_ref, wv_ref, query_ref, out_ref, prod):
+    chip = chip_ref[0]
+    at = pl.multiple_of(chip * 128, 128)
+    rows = wk_ref.shape[0]
+    q = query_ref[pl.ds(2 * chip, 2), :]
+    q2 = jnp.concatenate([q[0:1], q[1:2]], axis=1)
+    prod[...] = jnp.zeros(prod.shape, F32)
+    prod[0:rows, :] = wk_ref[:, pl.ds(at, 128)].astype(F32) * q2
+    sub, lane = iota((8, 128), 0), iota((8, 128), 1)
+    mine = jnp.where(lane // 64 == sub % 2, 1.0, 0.0)
+    fold = lax.dot_general(
+        mine, prod[...], (((1,), (1,)), ((), ())), precision=lax.Precision.HIGHEST, preferred_element_type=F32
+    )
+    top, mid, low = split3(fold)
+    part = jnp.where(sub < 2, top, jnp.where(sub < 4, mid, jnp.where(sub < 6, low, 0.0)))
+    both = jnp.concatenate([wv_ref[:, pl.ds(at, 128)].astype(F32), part], axis=0).astype(BF16)
     for d in range(out_ref.shape[0]):
         out_ref[d] = both
 
@@ -60,9 +73,9 @@
 
     slots = ids_ref.shape[1]
     rows[...] = jnp.zeros(rows.shape, F32)
-    sub = iota((8, 256), 0)
-    lane = iota((8, 256), 1)
-    meta = jnp.zeros((8, 256), F32)
+    sub = iota((8, 128), 0)
+    lane = iota((8, 128), 1)
+    meta = jnp.zeros((8, 128), F32)
     for s in range(slots):
         v = ids_ref[0, s]
         for k in range(4):
@@ -71,35 +84,49 @@
         meta = jnp.where((sub == s) & (lane == 48), v.astype(F32), meta)
     for i, (k, l) in enumerate(PAIRS):
         g = jnp.sum(rows[k] * rows[l], axis=-1, keepdims=True) * ((1.0 if k == l else 2.0) / width)
-        for part in range(3):
-            top = g.astype(BF16).astype(F32)
-            meta = jnp.where(lane == 16 * part + i, top, meta)
-            g = g - top
-    chunk[0 : 4 * slots, :] = pix_ref[...].astype(F32)
-    chunk[4 * slots :, :] = meta
-    packed = chunk[...].astype(BF16)
-    for j in range(send_ref.shape[0]):
-        send_ref[j] = packed
-
-
-def project_kernel(hi_ref, lo_ref, w_ref, thi_ref, tlo_ref):
-    w = w_ref[...]
-    t = jnp.dot(hi_ref[...], w, preferred_element_type=F32)
-    t = t + jnp.dot(lo_ref[...], w, preferred_element_type=F32)
-    hi = t.astype(BF16)
-    thi_ref[...] = hi
-    tlo_ref[...] = (t - hi.astype(F32)).astype(BF16)
-
-
-def attend_kernel(var_ref, count_ref, x_ref, thi_ref, tlo_ref, query_ref, out_ref, w_scr, v_scr):
-    head = var_ref[0]
+        for part, value in enumerate(split3(g)):
+            meta = jnp.where(lane == 16 * part + i, value, meta)
+    n = 4 * slots
+    for half in range(2):
+        chunk[32 * half : 32 * half + n, :] = pix_ref[:, 128 * half : 128 * half + 128].astype(F32)
+        chunk[32 * half + n : 32 * half + 32, :] = meta
+    send_ref[...] = chunk[...].astype(BF16)
+
+
+def project_kernel(hi_ref, lo_ref, both_ref, thi_ref, tlo_ref, key_ref, w_scr, f_scr):
+    n_dp = both_ref.shape[1]
+    rows = both_ref.shape[2] - 8
+    per = 128 // rows
+    for d in range(n_dp):
+        w_scr[d * rows : (d + 1) * rows, :] = both_ref[0, d, 0:rows, :]
+    for i in range(n_dp // per):
+        tile = jnp.zeros((8, 128), F32)
+        for p in range(per):
+            piece = both_ref[0, i * per + p, rows : rows + 8, :].astype(F32)
+            tile = tile + (pltpu.roll(piece, rows * p, 1) if p else piece)
+        f_scr[:, 128 * i : 128 * i + 128] = tile.astype(BF16)
+    hi, lo = hi_ref[...], lo_ref[...]
+    w, f = w_scr[...], f_scr[...]
+    t = jnp.dot(hi, w, preferred_element_type=F32) + jnp.dot(lo, w, preferred_element_type=F32)
+    top = t.astype(BF16)
+    thi_ref[...] = top
+    tlo_ref[...] = (t - top.astype(F32)).astype(BF16)
+    dims = (((1,), (1,)), ((), ()))
+    keys = lax.dot_general(f, hi, dims, preferred_element_type=F32)
+    keys = keys + lax.dot_general(f, lo, dims, preferred_element_type=F32)
+    key_ref[...] = keys + pltpu.roll(keys, 6, 0) + pltpu.roll(keys, 4, 0)
+
+
+def attend_kernel(half_ref, count_ref, both_ref, thi_ref, tlo_ref, key_ref, out_ref, w_scr, v_scr):
+    half = half_ref[0]
     count = count_ref[0]
-    half = head % 2
     slots = w_scr.shape[0] // 5
     entries = thi_ref.shape[0]
     n_pw = 364
     at = n_pw + 4
-    x = x_ref[...]
+    n_sv = slots // 6
+    x = both_ref[1, 0 : 64 * n_sv, :].reshape(n_sv, 2, 32, 128)
+    x = jnp.concatenate([x[:, i].reshape(32 * n_sv, 128) for i in range(2)], axis=1)
     n_rows = x.shape[0]
 
     n = iota((slots, n_rows), 0)
@@ -120,22 +147,22 @@
     col = iota((slots, entries), 1)
     lane = iota((slots, 128), 1)
     is_value = lane // 64 == half
-    q = query_ref[pl.ds(head, 1), :] * (1.0 / math.sqrt(query_ref.shape[1]))
-    q2 = jnp.concatenate([q, q], axis=1)
+    key_row = jnp.where(half == 0, key_ref[0:1, :], key_ref[1:2, :]) * 0.125
     thi, tlo = thi_ref[...], tlo_ref[...]
     keyed = []
     for k in range(5):
         target = 4 * ids + k if k < 4 else at + ids
-        pick = jnp.where(col == target, 1.0, 0.0).astype(BF16)
+        hit = col == target
+        keyed.append(jnp.sum(jnp.where(hit, key_row, 0.0), axis=1, keepdims=True))
+        pick = jnp.where(hit, 1.0, 0.0).astype(BF16)
         thi_k = jnp.dot(pick, thi, preferred_element_type=F32)
         t_k = thi_k + jnp.dot(pick, tlo, preferred_element_type=F32)
-        keyed.append(jnp.sum(jnp.where(is_value, 0.0, t_k * q2), axis=1, keepdims=True))
         v_scr[k * slots : (k + 1) * slots, :] = jnp.where(is_value, t_k, 0.0).astype(BF16)
     last = entries - 16
     tail = thi[last:, :].astype(F32) + tlo[last:, :].astype(F32)
     bias_row = tail[at + 91 - last : at + 92 - last, :]
     is_value_row = is_value[0:1, :]
-    key_bias = jnp.sum(jnp.where(is_value_row, 0.0, bias_row * q2), axis=1, keepdims=True)
+    key_bias = key_row[:, at + 91 : at + 92]
     value_bias = jnp.where(is_value_row, bias_row, 0.0)
 
     def g(k, l):
@@ -192,27 +219,30 @@
     slots, pp, patches = pixels.shape[1:]
     n_var, width = var_embed.shape
     n_dp = lax.axis_size(DP)
-    n_sv = lax.axis_size("var")
+    n_chip, n_core = lax.axis_size("y"), lax.axis_size("core")
+    n_sv = n_chip * n_core
     all_slots = slots * n_sv
     entries = 464
+    rows = key_weight.shape[0] + 8
     smem, vmem = whole(pltpu.SMEM), whole()
-    var = lax.axis_index("var").astype(jnp.int32).reshape(1)
+    chip = lax.axis_index("y").astype(jnp.int32).reshape(1)
+    core = lax.axis_index("core").astype(jnp.int32).reshape(1)
 
     slices = pl.pallas_call(
         head_slice_kernel,
-        out_shape=jax.ShapeDtypeStruct((n_dp, key_weight.shape[0], 128), BF16),
-        in_specs=[smem, vmem, vmem],
+        out_shape=jax.ShapeDtypeStruct((n_dp, rows, 128), BF16),
+        in_specs=[smem, vmem, vmem, vmem],
         out_specs=vmem,
+        scratch_shapes=[pltpu.VMEM((128, 128), F32)],
         name="head_slice",
-    )(var, key_weight, value_weight)
-    weights = lax.all_to_all(slices, DP, 0, 0, tiled=True)
-
-    hi, lo, send = pl.pallas_call(
+    )(chip, key_weight, value_weight, query)
+
+    hi, lo, packed = pl.pallas_call(
         table_kernel,
         out_shape=(
             jax.ShapeDtypeStruct((entries, width), BF16),
             jax.ShapeDtypeStruct((entries, width), BF16),
-            jax.ShapeDtypeStruct((n_sv, 32, patches), BF16),
+            jax.ShapeDtypeStruct((64, 128), BF16),
         ),
         in_specs=[smem] + [vmem] * 5,
         out_specs=(vmem, vmem, vmem),
@@ -220,7 +250,7 @@
             pltpu.VMEM((entries, width), F32),
             pltpu.VMEM((entries, width), F32),
             pltpu.VMEM((5, 8, width), F32),
-            pltpu.VMEM((32, patches), F32),
+            pltpu.VMEM((64, 128), F32),
         ],
         cost_estimate=cost(20 * entries * width, 8 * entries * width),
         compiler_params=pltpu.CompilerParams(vmem_limit_bytes=24 << 20),
@@ -233,18 +263,33 @@
         norm_gain.reshape(1, width),
         norm_bias.reshape(1, width),
     )
-    weights, send = lax.optimization_barrier((weights, send))
-    gathered = lax.all_to_all(send, "var", 0, 0, tiled=True)
-
-    thi, tlo = pl.pallas_call(
+    of_chip = lax.all_gather(packed, "core")
+
+    def weights_of_all(slices, of_chip):
+        return lax.all_to_all(slices, DP, 0, 0, tiled=True)
+
+    def pixels_of_all(slices, of_chip):
+        send = jnp.broadcast_to(of_chip, (n_chip, *of_chip.shape))
+        got = lax.all_to_all(send, "y", 0, 0, tiled=True).reshape(-1, 128)
+        return jnp.pad(got, ((0, n_dp * rows - got.shape[0]), (0, 0))).reshape(n_dp, rows, 128)
+
+    mine = lax.cond(core[0] == 0, weights_of_all, pixels_of_all, slices, of_chip)
+    both = lax.all_gather(mine, "core")
+
+    thi, tlo, keys = pl.pallas_call(
         project_kernel,
-        out_shape=(jax.ShapeDtypeStruct((entries, 128), BF16),) * 2,
+        out_shape=(
+            jax.ShapeDtypeStruct((entries, 128), BF16),
+            jax.ShapeDtypeStruct((entries, 128), BF16),
+            jax.ShapeDtypeStruct((8, entries), F32),
+        ),
         in_specs=[vmem] * 3,
-        out_specs=(vmem, vmem),
+        out_specs=(vmem, vmem, vmem),
+        scratch_shapes=[pltpu.VMEM((width, 128), BF16), pltpu.VMEM((8, width), BF16)],
         cost_estimate=cost(4 * entries * width * 128, 5 * entries * width),
         compiler_params=pltpu.CompilerParams(vmem_limit_bytes=16 << 20),
         name="project",
-    )(hi, lo, weights.reshape(width, 128))
+    )(hi, lo, both)
 
     mixed = pl.pallas_call(
         attend_kernel,
@@ -257,8 +302,8 @@
         ],
         compiler_params=pltpu.CompilerParams(vmem_limit_bytes=24 << 20),
         name="attend",
-    )(var, counts, gathered.reshape(n_sv * 32, patches), thi, tlo, query)
-    owned = lax.all_to_all(mixed.reshape(n_sv, patches // n_sv, 128), "var", 0, 0, tiled=True)
+    )(core, counts, both.reshape(n_core, n_dp * rows, 128), thi, tlo, keys)
+    owned = lax.all_to_all(mixed.reshape(n_sv, patches // n_sv, 128), VAR, 0, 0, tiled=True)
 
     out = pl.pallas_call(
         project_out_kernel,
@@ -272,13 +317,13 @@
 
 
 def solution(mesh):
-    torus = Mesh(mesh.devices.reshape(4, 8, mesh.shape["var"]), ("dp_0", "dp_1", "var"))
+    torus = Mesh(mesh.devices.reshape(4, 8, 8, 2), (*DP, *VAR))
     return jax.shard_map(
         on_device,
         mesh=torus,
         in_specs=(
-            P(DP, "var", None, None),
-            P(DP, "var"),
+            P(DP, VAR, None, None),
+            P(DP, VAR),
             P(DP),
             P(),
             P(),
@@ -289,6 +334,6 @@
             P(),
             P(),
         ),
-        out_specs=P(DP, "var", None),
+        out_specs=P(DP, VAR, None),
         check_vma=False,
     )

time: 60.8 us -> 56.6 us (0.931)
  blocking collectives: 10.5 us -> 44.4 us
  starting transfers between devices: 24.6 us -> 0 us
  waiting for transfers between devices: 12.1 us -> 0 us
  Pallas kernels: 6.58 us -> 5.75 us
    all_to_all x2 -> x0, starting transfers between devices: 24.6 us -> none  [the longest x1 13.7 us: on_device(): weights = lax.all_to_all(slices, DP, 0, 0, tiled=True)]
    all_gather x0 -> x2, blocking collectives: none -> 17.6 us  [the longest x1 9.2 us: on_device(): both = lax.all_gather(mine, 'core')]
    all_to_all x1 -> x2, blocking collectives: 10.5 us -> 26.8 us  [the longest x1 15.1 us: on_device(): lax.all_to_all(mixed.reshape(n_sv, patches // n_sv, 128), VAR, 0, 0, tile...]
    all_to_all x2 -> x0, waiting for transfers between devices: 12.1 us -> none  [the longest x1 8.01 us: on_device(): gathered = lax.all_to_all(send, 'var', 0, 0, tiled=True)]
    unnamed x22 -> x10, local copies, waits for them, and re-layouts: 4.33 us -> 2.96 us
    pallas_call x1, Pallas kernels: 1.99 us -> 1.27 us  [on_device(): pl.pallas_call(table_kernel, out_shape=(jax.ShapeDtypeStruct((entries, wi...]
    reshape x1, local copies, waits for them, and re-layouts: 0.01 us -> 0.72 us  [on_device(): pixels.reshape(slots * pp, patches)]
    pallas_call x1, Pallas kernels: 1.73 us -> 1.1 us  [on_device(): pl.pallas_call(head_slice_kernel, out_shape=jax.ShapeDtypeStruct((n_dp, r...]
  transfers between devices with their start and end apart: 2 -> 0, of which waited for: 2 -> 0; matrix products, arithmetic and copies ran while one was open for 3% -> 0% of each run, Pallas kernels for 4% -> 0%
where the time goes in v2:
time: 56.6 us; the launch traced here: 56.2 us
  blocking collectives  44.4 us (78%)
  Pallas kernels  5.75 us (10%)
  local copies, waits for them, and re-layouts  5.29 us (9%)
  between operations  0.7 us (1%)
    all_to_all x1, blocking collectives, on_device(): lax.all_to_all(mixed.reshape(n_sv, patches // n_sv, 128), VAR, 0, 0, tile...  15.1 us
    all_to_all x1, blocking collectives, pixels_of_all(): got = lax.all_to_all(send, 'y', 0, 0, tiled=True).reshape(-1, 128)  11.7 us
    all_gather x1, blocking collectives, on_device(): both = lax.all_gather(mine, 'core')  9.2 us
    all_gather x1, blocking collectives, on_device(): of_chip = lax.all_gather(packed, 'core')  8.37 us
    unnamed x10, local copies, waits for them, and re-layouts  2.96 us
    reshape x1, local copies, waits for them, and re-layouts, on_device(): patch_weight.reshape(n_var * pp, width)  1.54 us
    pallas_call x1, Pallas kernels, on_device(): pl.pallas_call(table_kernel, out_shape=(jax.ShapeDtypeStruct((entries, wi...  1.27 us
    pallas_call x1, Pallas kernels, on_device(): pl.pallas_call(attend_kernel, out_shape=jax.ShapeDtypeStruct((patches, 12...  1.21 us

profile of v2, /device:TPU:1, one launch (start us, length us, event | category | flops | bytes accessed | tf_op | source)
XLA Modules:
  0.0 56.2 jit_solution(2850142730610927056)
XLA Ops:
  0.0 1.5 %reshape.32.pw_ref = bf16[364,1024]{1,0:T(8,128)(2,1)S(1)} reshape(bf16[91,4,1024]{2,1,0:T(4,128)(2,1)} %param.16) | data formatting | bytes 1490944 | tf_op jit(solution)/shard_map/reshape | solution.py:261
  1.5 0.7 %reshape.31.pix_ref = bf16[24,256]{1,0:T(8,128)(2,1)S(1)} reshape(bf16[1,6,4,256]{3,2,1,0:T(4,128)(2,1)} %param.13) | data formatting | bytes 24576 | tf_op jit(solution)/shard_map/reshape | solution.py:260
  2.3 0.0 copy-start.1
  2.3 0.9 %copy-done.1 = bf16[91,1024]{1,0:T(8,128)(2,1)S(1)} copy-done((bf16[91,1024]{1,0:T(8,128)(2,1)S(1)}, bf16[91,1024]{1,0:T(8,128)(2,1)}, u32[]{:S(2)}) %copy-start.1) | copy-done | bytes 186392
  3.2 0.0 copy-start.2
  3.2 0.7 %copy-done.2 = f32[1024]{0:T(1024)S(1)} copy-done((f32[1024]{0:T(1024)S(1)}, f32[1024]{0:T(1024)}, u32[]{:S(2)}) %copy-start.2) | copy-done | bytes 4120
  3.9 0.0 copy-start.3
  3.9 0.7 %copy-done.3 = f32[1024]{0:T(1024)S(1)} copy-done((f32[1024]{0:T(1024)S(1)}, f32[1024]{0:T(1024)}, u32[]{:S(2)}) %copy-start.3) | copy-done | bytes 4120
  4.6 0.0 copy-start.4
  4.6 0.7 %copy-done.4 = s32[1,6]{1,0:T(1,128)S(1)} copy-done((s32[1,6]{1,0:T(1,128)S(1)}, s32[1,6]{1,0:T(1,128)}, u32[]{:S(2)}) %copy-start.4) | copy-done | bytes 48
  5.2 1.3 %tables.1 = (bf16[464,1024]{1,0:T(8,128)(2,1)S(1)}, bf16[464,1024]{1,0:T(8,128)(2,1)S(1)}, bf16[64,128]{1,0:T(8,128)(2,1)S(1)}) custom-call(s32[1,6]{1,0:T(1,128)S(1)} %copy-done.4, bf16[24,256]{1,0:T(8,128)(2,1)S(1)} %reshape.31.pix_ref, bf16[364,1024]{1,0:T(8,128)(2,1)S(1)} %reshape.32.pw_ref, bf16[91,1024]{1,0:T(8,128)(2,1)S(1)} %copy-done.1, ...), custom_call_target="tpu_custom_call" | custom-call | flops 9502720 | bytes 3801088 | tf_op jit(solution)/shard_map/tables/pallas_call | solution.py:240
  6.5 8.4 %all-gather = bf16[128,128]{1,0:T(8,128)(2,1)S(1)} all-gather(bf16[64,128]{1,0:T(8,128)(2,1)S(1)} %get-tuple-element.16), channel_id=2, replica_groups=mesh['dp_0'=4,'dp_1'=8,'y'=8,'core'=2] {'core'}, dimensions={0}, use_global_device_ids=true | all-gather | bytes 49152 | tf_op jit(solution)/shard_map/all_gather | solution.py:266
  14.9 1.1 %head_slice.1 = bf16[32,40,128]{2,1,0:T(8,128)(2,1)S(1)} custom-call(s32[1]{0:T(128)} %bitcast.6.chip_ref, bf16[32,1024]{1,0:T(8,128)(2,1)} %wk_ref.1, bf16[32,1024]{1,0:T(8,128)(2,1)} %wv_ref.1, f32[16,64]{1,0:T(8,128)} %query_ref.1), custom_call_target="tpu_custom_call" | custom-call | tf_op jit(solution)/shard_map/head_slice/pallas_call | solution.py:231
  16.0 11.8 %conditional.1 = (bf16[32,40,128]{2,1,0:T(8,128)(2,1)S(1)}) conditional(s32[]{:T(128)} %convert_element_type.5, (bf16[128,128]{1,0:T(8,128)(2,1)S(1)}) %tuple.11, bf16[32,40,128]{2,1,0:T(8,128)(2,1)S(1)} %head_slice.1), branch_computations={%region_0.1_spmd, %region_1.2_spmd} | conditional | bytes 1409034 | solution.py:276
  16.0 11.7 %all_to_all.13 = bf16[8,2,64,128]{3,2,1,0:T(8,128)(2,1)S(1)} all-to-all(bf16[8,2,64,128]{3,2,1,0:T(8,128)(2,1)S(1)} %broadcast_in_dim.4), channel_id=1, replica_groups=mesh['dp_0'=4,'dp_1'=8,'y'=8,'core'=2] {'y'}, dimensions={0} | all-to-all | bytes 524288 | tf_op jit(solution)/shard_map/cond/branch_0_fun/all_to_all | solution.py:273
  27.8 0.0 copy-start
  27.8 9.2 %all-gather.1 = bf16[64,40,128]{2,1,0:T(8,128)(2,1)S(1)} all-gather(bf16[32,40,128]{2,1,0:T(8,128)(2,1)S(1)} %get-tuple-element.23), channel_id=3, replica_groups=mesh['dp_0'=4,'dp_1'=8,'y'=8,'core'=2] {'core'}, dimensions={0}, use_global_device_ids=true | all-gather | bytes 983040 | tf_op jit(solution)/shard_map/all_gather | solution.py:277
  37.7 1.2 %project.1 = (bf16[464,128]{1,0:T(8,128)(2,1)S(1)}, bf16[464,128]{1,0:T(8,128)(2,1)S(1)}, f32[8,464]{1,0:T(8,128)S(1)}) custom-call(bf16[464,1024]{1,0:T(8,128)(2,1)S(1)} %get-tuple-element.17.hi_ref, bf16[464,1024]{1,0:T(8,128)(2,1)S(1)} %get-tuple-element.18.lo_ref, bf16[2,32,40,128]{3,2,1,0:T(8,128)(2,1)S(1)} %bitcast.11), custom_call_target="tpu_custom_call" | custom-call | flops 243269632 | bytes 2375680 | tf_op jit(solution)/shard_map/project/pallas_call | solution.py:279
  38.9 1.2 %attend.1 = bf16[256,128]{1,0:T(8,128)(2,1)S(1)} custom-call(s32[1]{0:T(128)} %bitcast.3.half_ref, s32[1]{0:T(128)S(6)} %copy.14.count_ref, bf16[2,1280,128]{2,1,0:T(8,128)(2,1)S(1)} %bitcast.12, bf16[464,128]{1,0:T(8,128)(2,1)S(1)} %get-tuple-element.19.thi_ref, bf16[464,128]{1,0:T(8,128)(2,1)S(1)} %get-tuple-element.20.tlo_ref, ...), custom_call_target="tpu_custom_call" | custom-call | tf_op jit(solution)/shard_map/attend/pallas_call | solution.py:294
  40.1 15.1 %all_to_all.15.m_ref = bf16[16,16,128]{2,1,0:T(8,128)(2,1)S(1)} all-to-all(bf16[16,16,128]{2,1,0:T(8,128)(2,1)S(1)} %bitcast.13), channel_id=1, replica_groups=mesh['dp_0'=4,'dp_1'=8,'y'=8,'core'=2] {'y','core'}, dimensions={0} | all-to-all | bytes 131072 | tf_op jit(solution)/shard_map/all_to_all | solution.py:306
  55.1 0.0 copy-done
  55.2 1.0 %project_out.1 = bf16[16,1024]{1,0:T(8,128)(2,1)} custom-call(bf16[16,16,128]{2,1,0:T(8,128)(2,1)S(1)} %all_to_all.15.m_ref, bf16[1024,1024]{1,0:T(8,128)(2,1)S(1)} %copy-done), custom_call_target="tpu_custom_call" | custom-call | tf_op jit(solution)/shard_map/project_out/pallas_call | solution.py:308
  (2 shorter events, 0.1 us)
Async XLA Ops:
  2.3 0.9 %copy-start.1 = (bf16[91,1024]{1,0:T(8,128)(2,1)S(1)}, bf16[91,1024]{1,0:T(8,128)(2,1)}, u32[]{:S(2)}) copy-start(bf16[91,1024]{1,0:T(8,128)(2,1)} %ve_ref.1) | copy-start | bytes 559108
  3.2 0.7 %copy-start.2 = (f32[1024]{0:T(1024)S(1)}, f32[1024]{0:T(1024)}, u32[]{:S(2)}) copy-start(f32[1024]{0:T(1024)} %param.18) | copy-start | bytes 12292
  3.9 0.7 %copy-start.3 = (f32[1024]{0:T(1024)S(1)}, f32[1024]{0:T(1024)}, u32[]{:S(2)}) copy-start(f32[1024]{0:T(1024)} %param.19) | copy-start | bytes 12292
  4.6 0.7 %copy-start.4 = (s32[1,6]{1,0:T(1,128)S(1)}, s32[1,6]{1,0:T(1,128)}, u32[]{:S(2)}) copy-start(s32[1,6]{1,0:T(1,128)} %ids_ref.1) | copy-start | bytes 76
  27.8 27.3 %copy-start = (bf16[1024,1024]{1,0:T(8,128)(2,1)S(1)}, bf16[1024,1024]{1,0:T(8,128)(2,1)}, u32[]{:S(2)}) copy-start(bf16[1024,1024]{1,0:T(8,128)(2,1)} %wo_ref.1) | copy-start | bytes 6291460

commit v3 on v2

v3 whole, which is shorter than its diff:
```python
import jax
import jax.numpy as jnp
from jax import lax
from jax.experimental import pallas as pl
from jax.experimental.pallas import tpu as pltpu
from jax.sharding import Mesh
from jax.sharding import PartitionSpec as P

DP = ("dp_0", "dp_1")
VAR = ("y", "core")
F32 = jnp.float32
BF16 = jnp.bfloat16
NT = (((1,), (1,)), ((), ()))
TN = (((0,), (0,)), ((), ()))
PAIRS = [(k, l) for k in range(5) for l in range(k, 5)]


def whole(memory_space=pltpu.VMEM):
    return pl.BlockSpec(memory_space=memory_space)


def iota(shape, dim):
    return lax.broadcasted_iota(jnp.int32, shape, dim)


def split3(x):
    top = x.astype(BF16).astype(F32)
    mid = (x - top).astype(BF16).astype(F32)
    return top, mid, (x - top - mid).astype(BF16).astype(F32)


def pack_kernel(chip_ref, ids_ref, wk_ref, wv_ref, query_ref, pix_ref, w_ref, send_ref, wk, wv, q_scr, pix, prod, chunk, sems):
    chip = chip_ref[0]
    at = pl.multiple_of(chip * 128, 128)
    copies = [
        pltpu.make_async_copy(pix_ref, pix, sems.at[0]),
        pltpu.make_async_copy(query_ref, q_scr, sems.at[1]),
        pltpu.make_async_copy(wk_ref.at[:, pl.ds(at, 128)], wk, sems.at[2]),
        pltpu.make_async_copy(wv_ref.at[:, pl.ds(at, 128)], wv, sems.at[3]),
    ]
    for copy in copies:
        copy.start()
    rows = wk.shape[0]
    slots = ids_ref.shape[1]
    prod[...] = jnp.zeros(prod.shape, F32)
    sub, lane = iota((8, 128), 0), iota((8, 128), 1)
    mine = jnp.where(lane // 64 == sub % 2, 1.0, 0.0)
    meta = jnp.zeros((8, 128), F32)
    for s in range(slots):
        meta = jnp.where(sub == s, ids_ref[0, s].astype(F32), meta)
    n = 4 * slots
    for half in range(2):
        chunk[32 * half + n : 32 * half + 32, :] = meta
    copies[0].wait()
    for s in range(slots):
        x = pix[0, s].astype(F32)
        for half in range(2):
            chunk[32 * half + 4 * s : 32 * half + 4 * s + 4, :] = x[:, 128 * half : 128 * half + 128]
    send_ref[...] = chunk[...].astype(BF16)

    for copy in copies[1:]:
        copy.wait()
    q = q_scr[pl.ds(2 * chip, 2), :]
    prod[0:rows, :] = wk[...].astype(F32) * jnp.concatenate([q[0:1], q[1:2]], axis=1)
    fold = lax.dot_general(mine, prod[...], NT, precision=lax.Precision.HIGHEST, preferred_element_type=F32)
    top, mid, low = split3(fold)
    part = jnp.where(sub < 2, top, jnp.where(sub < 4, mid, jnp.where(sub < 6, low, 0.0)))
    w_ref[...] = jnp.concatenate([wv[...].astype(F32), part], axis=0).astype(BF16)


def table_kernel(pw_ref, ve_ref, gain_ref, bias_ref, hi_ref, lo_ref, gram_ref, ac, af):
    n_pw, width = pw_ref.shape
    n_ve = ve_ref.shape[0]
    total = af.shape[0]
    at = n_pw + 4
    gain = gain_ref[...]

    def centered(x):
        return x - jnp.mean(x, axis=-1, keepdims=True)

    pw = centered(pw_ref[...].astype(F32))
    tiles = width // 128
    for i in range(tiles):
        ac[i, 0:n_pw, :] = pw[:, 128 * i : 128 * i + 128]
    af[0:n_pw, :] = pw * gain
    af[n_pw:at, :] = jnp.zeros((at - n_pw, width), F32)
    ve = centered(ve_ref[...].astype(F32))
    af[at : at + n_ve, :] = ve * gain
    af[at + n_ve : at + n_ve + 1, :] = bias_ref[...]
    af[at + n_ve + 1 : total, :] = jnp.zeros((total - at - n_ve - 1, width), F32)
    a = af[...]
    hi = a.astype(BF16)
    hi_ref[...] = hi
    lo_ref[...] = (a - hi.astype(F32)).astype(BF16)

    sums = [jnp.zeros((n_ve, 128), F32) for _ in PAIRS]
    for i in range(tiles):
        planes = [ac[i, pl.ds(k, n_ve, stride=4), :] for k in range(4)] + [ve[:, 128 * i : 128 * i + 128]]
        sums = [total + planes[k] * planes[l] for total, (k, l) in zip(sums, PAIRS, strict=True)]
    lane = iota((n_ve, 128), 1)
    gram = jnp.zeros((n_ve, 128), F32)
    for i, (k, l) in enumerate(PAIRS):
        g = jnp.sum(sums[i], axis=-1, keepdims=True) * ((1.0 if k == l else 2.0) / width)
        gram = jnp.where(lane == i, g, gram)
    top, mid, low = split3(gram)
    gram = top + pltpu.roll(mid, 16, 1) + pltpu.roll(low, 32, 1)
    gram_ref[...] = jnp.zeros(gram_ref.shape, BF16)
    gram_ref[0:n_ve, :] = gram.astype(BF16)


def attend_kernel(core_ref, count_ref, hi_ref, lo_ref, gram_ref, both_ref, out_ref, wv_scr, f_scr, w_scr, v_scr):
    half = core_ref[0]
    count = count_ref[0]
    n_dp = both_ref.shape[1]
    rows = both_ref.shape[2] - 8
    per = 128 // rows
    for d in range(n_dp):
        wv_scr[d * rows : (d + 1) * rows, :] = both_ref[0, d, 0:rows, :]
    for i in range(n_dp // per):
        tile = jnp.zeros((8, 128), F32)
        for p in range(per):
            piece = both_ref[0, i * per + p, rows : rows + 8, :].astype(F32)
            tile = tile + (pltpu.roll(piece, rows * p, 1) if p else piece)
        f_scr[:, 128 * i : 128 * i + 128] = tile.astype(BF16)
    hi, lo = hi_ref[...], lo_ref[...]
    wv, f = wv_scr[...], f_scr[...]
    t = jnp.dot(hi, wv, preferred_element_type=F32) + jnp.dot(lo, wv, preferred_element_type=F32)
    thi = t.astype(BF16)
    tlo = (t - thi.astype(F32)).astype(BF16)
    keys = lax.dot_general(f, hi, NT, preferred_element_type=F32)
    keys = keys + lax.dot_general(f, lo, NT, preferred_element_type=F32)
    keys = (keys + pltpu.roll(keys, 6, 0) + pltpu.roll(keys, 4, 0)) * 0.125
    key_row = jnp.where(half == 0, keys[0:1], keys[1:2])

    slots = w_scr.shape[0] // 5
    entries = hi_ref.shape[0]
    n_ve = gram_ref.shape[0]
    at = entries - n_ve
    n_sv = slots // 6
    x = both_ref[1].reshape(n_dp * (rows + 8), 128)[0 : 64 * n_sv, :].reshape(n_sv, 2, 32, 128)
    x = jnp.concatenate([x[:, i].reshape(32 * n_sv, 128) for i in range(2)], axis=1)
    n_rows = x.shape[0]
    n = iota((slots, n_rows), 0)
    group = (n * 43) >> 8
    base = group * 32
    within = n - group * 6
    col = iota((slots, n_rows), 1)

    def picked(hit):
        return jnp.where(hit, 1.0, 0.0).astype(BF16)

    meta = jnp.dot(picked(col == base + 24 + within), x[:, :128], preferred_element_type=F32)
    c = [jnp.dot(picked(col == base + within * 4 + k), x, preferred_element_type=F32) for k in range(4)]
    ids = meta[:, 0:1].astype(jnp.int32)
    gram = jnp.dot(picked(iota((slots, n_ve), 1) == ids), gram_ref[...], preferred_element_type=F32)
    gram = gram + pltpu.roll(gram, 112, 1) + pltpu.roll(gram, 96, 1)

    col = iota((slots, entries), 1)
    is_value = iota((slots, 128), 1) // 64 == half
    keyed = []
    for k in range(5):
        hit = col == (4 * ids + k if k < 4 else at + ids)
        keyed.append(jnp.sum(jnp.where(hit, key_row, 0.0), axis=1, keepdims=True))
        v = jnp.dot(picked(hit), thi, preferred_element_type=F32)
        v_scr[k * slots : (k + 1) * slots, :] = jnp.where(is_value, v, 0.0).astype(BF16)
    bias_row = t[at + 91 : at + 92, :]
    key_bias = key_row[:, at + 91 : at + 92]
    value_bias = jnp.where(is_value[0:1, :], bias_row, 0.0)

    def g(k, l):
        i = PAIRS.index((k, l))
        return gram[:, i : i + 1]

    spread = g(4, 4)
    for k in range(4):
        inner = g(k, 4)
        for l in range(k, 4):
            inner = inner + g(k, l) * c[l]
        spread = spread + c[k] * inner
    r = lax.rsqrt(jnp.maximum(spread, 0.0) + 1e-05)
    dots = keyed[4]
    for k in range(4):
        dots = dots + c[k] * keyed[k]
    scores = r * dots + key_bias
    scores = jnp.where(iota(scores.shape, 0) < count, scores, -1e30)
    peak = jnp.max(scores, axis=0, keepdims=True)
    expo = jnp.exp(scores - peak)
    share = expo * (1.0 / jnp.sum(expo, axis=0, keepdims=True)) * r
    for k in range(4):
        w_scr[k * slots : (k + 1) * slots, :] = (share * c[k]).astype(BF16)
    w_scr[4 * slots :, :] = share.astype(BF16)
    mixed = lax.dot_general(w_scr[...], v_scr[...], TN, preferred_element_type=F32)
    out_ref[...] = (mixed + value_bias).astype(BF16)


def project_out_kernel(m_ref, wo_ref, out_ref):
    parts = [m_ref[2 * i].astype(F32) + m_ref[2 * i + 1].astype(F32) for i in range(m_ref.shape[0] // 2)]
    mixed = jnp.concatenate(parts, axis=1).astype(BF16)
    out_ref[...] = jnp.dot(mixed, wo_ref[...], preferred_element_type=F32).astype(BF16)


def cost(flops, moved):
    return pl.CostEstimate(flops=flops, transcendentals=0, bytes_accessed=moved)


def on_device(
    pixels,
    var_ids,
    counts,
    patch_weight,
    var_embed,
    norm_gain,
    norm_bias,
    key_weight,
    value_weight,
    query,
    out_weight,
):
    slots, pp, patches = pixels.shape[1:]
    n_var, width = var_embed.shape
    n_dp = lax.axis_size(DP)
    n_chip, n_core = lax.axis_size("y"), lax.axis_size("core")
    n_sv = n_chip * n_core
    all_slots = slots * n_sv
    entries = 464
    rows = key_weight.shape[0] + 8
    smem, vmem = whole(pltpu.SMEM), whole()
    chip = lax.axis_index("y").astype(jnp.int32).reshape(1)
    core = lax.axis_index("core").astype(jnp.int32).reshape(1)

    packed_w, packed_x = pl.pallas_call(
        pack_kernel,
        out_shape=(jax.ShapeDtypeStruct((rows, 128), BF16), jax.ShapeDtypeStruct((64, 128), BF16)),
        in_specs=[smem, smem] + [whole(pltpu.HBM)] * 4,
        out_specs=(vmem, vmem),
        scratch_shapes=[
            pltpu.VMEM((rows - 8, 128), BF16),
            pltpu.VMEM((rows - 8, 128), BF16),
            pltpu.VMEM(query.shape, F32),
            pltpu.VMEM(pixels.shape, BF16),
            pltpu.VMEM((128, 128), F32),
            pltpu.VMEM((64, 128), F32),
            pltpu.SemaphoreType.DMA((4,)),
        ],
        name="pack",
    )(chip, var_ids, key_weight, value_weight, query, pixels)
    of_chip = lax.all_gather(packed_x, "core")

    def tables(patch_weight, var_embed, norm_gain, norm_bias):
        return pl.pallas_call(
            table_kernel,
            out_shape=(
                jax.ShapeDtypeStruct((entries, width), BF16),
                jax.ShapeDtypeStruct((entries, width), BF16),
                jax.ShapeDtypeStruct((96, 128), BF16),
            ),
            in_specs=[vmem] * 4,
            out_specs=(vmem,) * 3,
            scratch_shapes=[pltpu.VMEM((width // 128, n_var * pp + 4, 128), F32), pltpu.VMEM((entries, width), F32)],
            cost_estimate=cost(20 * entries * width, 8 * entries * width),
            compiler_params=pltpu.CompilerParams(vmem_limit_bytes=24 << 20),
            name="tables",
        )(
            patch_weight.reshape(n_var * pp, width),
            var_embed,
            norm_gain.reshape(1, width),
            norm_bias.reshape(1, width),
        )

    def weights_of_all(packed_w, of_chip, *params):
        send = jnp.broadcast_to(packed_w, (n_dp, *packed_w.shape))
        return lax.all_to_all(send, DP, 0, 0, tiled=True), *tables(*params)

    def pixels_of_all(packed_w, of_chip, *params):
        send = jnp.broadcast_to(of_chip, (n_chip, *of_chip.shape))
        got = lax.all_to_all(send, "y", 0, 0, tiled=True).reshape(-1, 128)
        got = jnp.pad(got, ((0, n_dp * rows - got.shape[0]), (0, 0))).reshape(n_dp, rows, 128)
        return got, *tables(*params)

    params = (patch_weight, var_embed, norm_gain, norm_bias)
    mine, hi, lo, gram = lax.cond(core[0] == 0, weights_of_all, pixels_of_all, packed_w, of_chip, *params)
    both = lax.all_gather(mine, "core")

    mixed = pl.pallas_call(
        attend_kernel,
        out_shape=jax.ShapeDtypeStruct((patches, 128), BF16),
        in_specs=[smem, smem] + [vmem] * 4,
        out_specs=vmem,
        scratch_shapes=[
            pltpu.VMEM((width, 128), BF16),
            pltpu.VMEM((8, width), BF16),
            pltpu.VMEM((5 * all_slots, patches), BF16),
            pltpu.VMEM((5 * all_slots, 128), BF16),
        ],
        compiler_params=pltpu.CompilerParams(vmem_limit_bytes=24 << 20),
        name="attend",
    )(core, counts, hi, lo, gram, both)
    owned = lax.all_to_all(mixed.reshape(n_sv, patches // n_sv, 128), VAR, 0, 0, tiled=True)

    out = pl.pallas_call(
        project_out_kernel,
        out_shape=jax.ShapeDtypeStruct((patches // n_sv, width), BF16),
        in_specs=[vmem, vmem],
        out_specs=vmem,
        compiler_params=pltpu.CompilerParams(vmem_limit_bytes=16 << 20),
        name="project_out",
    )(owned, out_weight)
    return out[None]


def solution(mesh):
    torus = Mesh(mesh.devices.reshape(4, 8, 8, 2), (*DP, *VAR))
    return jax.shard_map(
        on_device,
        mesh=torus,
        in_specs=(
            P(DP, VAR, None, None),
            P(DP, VAR),
            P(DP),
            P(),
            P(),
            P(),
            P(),
            P(DP, None),
            P(DP, None),
            P(),
            P(),
        ),
        out_specs=P(DP, VAR, None),
        check_vma=False,
    )
```

time: 56.6 us -> 52.4 us (0.926)
  blocking collectives: 44.4 us -> 31.9 us
  waiting for transfers between devices: 0 us -> 6.29 us
  starting transfers between devices: 0 us -> 3.41 us
  local copies, waits for them, and re-layouts: 5.29 us -> 3.06 us
  Pallas kernels: 5.75 us -> 6.67 us
    all_to_all x1 -> x0, blocking collectives: 11.7 us -> none  [pixels_of_all(): got = lax.all_to_all(send, 'y', 0, 0, tiled=True).reshape(-1, 128)]
    all_to_all x0 -> x1, waiting for transfers between devices: none -> 6.29 us  [pixels_of_all(): got = lax.all_to_all(send, 'y', 0, 0, tiled=True).reshape(-1, 128)]
    all_to_all x0 -> x1, starting transfers between devices: none -> 3.41 us  [pixels_of_all(): got = lax.all_to_all(send, 'y', 0, 0, tiled=True).reshape(-1, 128)]
    unnamed x10 -> x2, local copies, waits for them, and re-layouts: 2.96 us -> 0.01 us
    pallas_call x1, Pallas kernels: 1.21 us -> 2.25 us  [on_device(): pl.pallas_call(attend_kernel, out_shape=jax.ShapeDtypeStruct((patches, 12...]
    all_gather x1, blocking collectives: 9.2 us -> 8.19 us  [on_device(): both = lax.all_gather(mine, 'core')]
    pad x1, local copies, waits for them, and re-layouts: 0.03 us -> 0.75 us  [pixels_of_all(): jnp.pad(got, ((0, n_dp * rows - got.shape[0]), (0, 0)))]
    reshape x2 -> x1, local copies, waits for them, and re-layouts: 2.26 us -> 1.55 us  [tables(): patch_weight.reshape(n_var * pp, width)]
  transfers between devices with their start and end apart: 0 -> 1, of which waited for: 0 -> 1; matrix products, arithmetic and copies ran while one was open for 0% -> 3% of each run, Pallas kernels for 0% -> 3%
where the time goes in v3:
time: 52.4 us; the launch traced here: 52 us
  blocking collectives  31.9 us (61%)
  Pallas kernels  6.67 us (13%)
  waiting for transfers between devices  6.29 us (12%)
  starting transfers between devices  3.41 us (7%)
  local copies, waits for them, and re-layouts  3.06 us (6%)
  between operations  0.67 us (1%)
    all_to_all x1, blocking collectives, on_device(): lax.all_to_all(mixed.reshape(n_sv, patches // n_sv, 128), VAR, 0, 0, tile...  15.1 us
    all_gather x1, blocking collectives, on_device(): of_chip = lax.all_gather(packed_x, 'core')  8.58 us
    all_gather x1, blocking collectives, on_device(): both = lax.all_gather(mine, 'core')  8.19 us
    all_to_all x1, waiting for transfers between devices, pixels_of_all(): got = lax.all_to_all(send, 'y', 0, 0, tiled=True).reshape(-1, 128)  6.29 us
    all_to_all x1, starting transfers between devices, pixels_of_all(): got = lax.all_to_all(send, 'y', 0, 0, tiled=True).reshape(-1, 128)  3.41 us
    pallas_call x1, Pallas kernels, on_device(): pl.pallas_call(attend_kernel, out_shape=jax.ShapeDtypeStruct((patches, 12...  2.25 us
    pallas_call x1, Pallas kernels, on_device(): pl.pallas_call(pack_kernel, out_shape=(jax.ShapeDtypeStruct((rows, 128),...  2.05 us
    reshape x1, local copies, waits for them, and re-layouts, tables(): patch_weight.reshape(n_var * pp, width)  1.55 us
  transfers between devices with their start and end apart: 1, of which 1 were waited for; matrix products, arithmetic and copies ran while one was open for 3% of the time, Pallas kernels for 3%

profile of v3, /device:TPU:1, one launch (start us, length us, event | category | flops | bytes accessed | tf_op | source)
XLA Modules:
  0.0 52.0 jit_solution(17709560961390215499)
XLA Ops:
  0.0 2.0 %pack.1 = (bf16[40,128]{1,0:T(8,128)(2,1)S(1)}, bf16[64,128]{1,0:T(8,128)(2,1)}) custom-call(s32[1]{0:T(128)} %bitcast.8.chip_ref, s32[1,6]{1,0:T(1,128)} %ids_ref.1, bf16[32,1024]{1,0:T(8,128)(2,1)} %wk_ref.1, bf16[32,1024]{1,0:T(8,128)(2,1)} %wv_ref.1, f32[16,64]{1,0:T(8,128)} %query_ref.1, bf16[1,6,4,256]{3,2,1,0:T(4,128)(2,1)} %pix_ref.1), custom_call_target="tpu_custom_call" | custom-call | tf_op jit(solution)/shard_map/pack/pallas_call | solution.py:231
  2.1 8.6 %all-gather = bf16[128,128]{1,0:T(8,128)(2,1)S(1)} all-gather(bf16[64,128]{1,0:T(8,128)(2,1)} %get-tuple-element.47), channel_id=2, replica_groups=mesh['dp_0'=4,'dp_1'=8,'y'=8,'core'=2] {'core'}, dimensions={0}, use_global_device_ids=true | all-gather | bytes 49152 | tf_op jit(solution)/shard_map/all_gather | solution.py:247
  10.6 14.2 %conditional.1 = (bf16[32,40,128]{2,1,0:T(8,128)(2,1)}, bf16[464,1024]{1,0:T(8,128)(2,1)S(1)}, bf16[464,1024]{1,0:T(8,128)(2,1)S(1)}, bf16[96,128]{1,0:T(8,128)(2,1)S(1)}) conditional(s32[]{:T(128)} %convert_element_type.5, (bf16[128,128]{1,0:T(8,128)(2,1)S(1)}, bf16[91,4,1024]{2,1,0:T(4,128)(2,1)}, f32[1024]{0:T(1024)}, f32[1024]{0:T(1024)}, ...), branch_computations={%region_0.1_spmd, %region_1.2_spmd} | conditional | flops 9502720 | bytes 7741590 | solution.py:281
  10.6 0.0 copy-start.1
  10.6 0.0 copy-start.3
  10.6 0.0 copy-start.5
  10.6 0.7 %broadcast_in_dim.6 = bf16[8,2,64,128]{3,2,1,0:T(8,128)(2,1)} broadcast(bf16[2,64,128]{2,1,0:T(8,128)(2,1)S(1)} %bitcast.15), dimensions={1,2,3} | broadcast | bytes 294912 | tf_op jit(solution)/shard_map/cond/branch_0_fun/broadcast_in_dim | solution.py:275
  11.4 3.4 %all-to-all-start = ((bf16[8,2,64,128]{3,2,1,0:T(8,128)(2,1)}), bf16[8,2,64,128]{3,2,1,0:T(8,128)(2,1)S(1)}, u32[]{:S(2)}, u32[]{:S(2)}) async-start(bf16[8,2,64,128]{3,2,1,0:T(8,128)(2,1)} %broadcast_in_dim.6), calls=%async_computation | async-start | bytes 524288 | tf_op jit(solution)/shard_map/cond/branch_0_fun/all_to_all | solution.py:276
  14.8 1.5 %reshape.24.pw_ref = bf16[364,1024]{1,0:T(8,128)(2,1)S(1)} reshape(bf16[91,4,1024]{2,1,0:T(4,128)(2,1)} %get-tuple-element.26) | data formatting | bytes 1490944 | tf_op jit(solution)/shard_map/cond/branch_0_fun/reshape | solution.py:264
  16.4 0.0 copy-done.1
  16.4 0.0 copy-done.3
  16.4 0.0 copy-done.5
  16.4 1.4 %tables.2 = (bf16[464,1024]{1,0:T(8,128)(2,1)S(1)}, bf16[464,1024]{1,0:T(8,128)(2,1)S(1)}, bf16[96,128]{1,0:T(8,128)(2,1)S(1)}) custom-call(bf16[364,1024]{1,0:T(8,128)(2,1)S(1)} %reshape.24.pw_ref, bf16[91,1024]{1,0:T(8,128)(2,1)S(1)} %copy-done.1, f32[1,1024]{1,0:T(1,128)S(1)} %bitcast.16, f32[1,1024]{1,0:T(1,128)S(1)} %bitcast.18), custom_call_target="tpu_custom_call" | custom-call | flops 9502720 | bytes 3801088 | tf_op jit(solution)/shard_map/cond/branch_0_fun/tables/pallas_call | solution.py:250
  17.8 6.3 %all-to-all-done = bf16[8,2,64,128]{3,2,1,0:T(8,128)(2,1)S(1)} async-done(((bf16[8,2,64,128]{3,2,1,0:T(8,128)(2,1)}), bf16[8,2,64,128]{3,2,1,0:T(8,128)(2,1)S(1)}, u32[]{:S(2)}, u32[]{:S(2)}) %all-to-all-start) | async-done | bytes 262176 | tf_op jit(solution)/shard_map/cond/branch_0_fun/all_to_all | solution.py:276
  24.1 0.8 %pad.3 = bf16[1280,128]{1,0:T(8,128)(2,1)} pad(bf16[1024,128]{1,0:T(8,128)(2,1)S(1)} %bitcast.14, bf16[]{:T(256)} %constant.4.clone), padding=0_256x0_0 | pad | bytes 589826 | tf_op jit(solution)/shard_map/cond/branch_0_fun/jit(_pad)/pad | solution.py:277
  24.8 0.0 copy-start
  24.8 8.2 %all-gather.1 = bf16[64,40,128]{2,1,0:T(8,128)(2,1)S(1)} all-gather(bf16[32,40,128]{2,1,0:T(8,128)(2,1)} %get-tuple-element.52), channel_id=3, replica_groups=mesh['dp_0'=4,'dp_1'=8,'y'=8,'core'=2] {'core'}, dimensions={0}, use_global_device_ids=true | all-gather | bytes 983040 | tf_op jit(solution)/shard_map/all_gather | solution.py:282
  33.7 2.2 %attend.1 = bf16[256,128]{1,0:T(8,128)(2,1)S(1)} custom-call(s32[1]{0:T(128)} %bitcast.7.core_ref, s32[1]{0:T(128)S(6)} %copy.20.count_ref, bf16[464,1024]{1,0:T(8,128)(2,1)S(1)} %get-tuple-element.49.hi_ref, bf16[464,1024]{1,0:T(8,128)(2,1)S(1)} %get-tuple-element.50.lo_ref, bf16[96,128]{1,0:T(8,128)(2,1)S(1)} %get-tuple-element.51.gram_ref, ...), custom_call_target="tpu_custom_call" | custom-call | tf_op jit(solution)/shard_map/attend/pallas_call | solution.py:284
  35.9 15.1 %all_to_all.13.m_ref = bf16[16,16,128]{2,1,0:T(8,128)(2,1)S(1)} all-to-all(bf16[16,16,128]{2,1,0:T(8,128)(2,1)S(1)} %bitcast.13), channel_id=1, replica_groups=mesh['dp_0'=4,'dp_1'=8,'y'=8,'core'=2] {'y','core'}, dimensions={0} | all-to-all | bytes 131072 | tf_op jit(solution)/shard_map/all_to_all | solution.py:298
  51.0 0.0 copy-done
  51.0 1.0 %project_out.1 = bf16[16,1024]{1,0:T(8,128)(2,1)} custom-call(bf16[16,16,128]{2,1,0:T(8,128)(2,1)S(1)} %all_to_all.13.m_ref, bf16[1024,1024]{1,0:T(8,128)(2,1)S(1)} %copy-done), custom_call_target="tpu_custom_call" | custom-call | tf_op jit(solution)/shard_map/project_out/pallas_call | solution.py:300
Async XLA Ops:
  10.6 5.7 %copy-start.1 = (bf16[91,1024]{1,0:T(8,128)(2,1)S(1)}, bf16[91,1024]{1,0:T(8,128)(2,1)}, u32[]{:S(2)}) copy-start(bf16[91,1024]{1,0:T(8,128)(2,1)} %get-tuple-element.27.ve_ref) | copy-start | bytes 559108 | tf_op jit(solution)/shard_map/cond
  10.6 5.7 %copy-start.3 = (f32[1024]{0:T(1024)S(1)}, f32[1024]{0:T(1024)}, u32[]{:S(2)}) copy-start(f32[1024]{0:T(1024)} %get-tuple-element.28) | copy-start | bytes 12292 | tf_op jit(solution)/shard_map/cond
  10.6 5.7 %copy-start.5 = (f32[1024]{0:T(1024)S(1)}, f32[1024]{0:T(1024)}, u32[]{:S(2)}) copy-start(f32[1024]{0:T(1024)} %get-tuple-element.29) | copy-start | bytes 12292 | tf_op jit(solution)/shard_map/cond
  11.4 12.7 %all-to-all-start = ((bf16[8,2,64,128]{3,2,1,0:T(8,128)(2,1)}), bf16[8,2,64,128]{3,2,1,0:T(8,128)(2,1)S(1)}, u32[]{:S(2)}, u32[]{:S(2)}) async-start(bf16[8,2,64,128]{3,2,1,0:T(8,128)(2,1)} %broadcast_in_dim.6), calls=%async_computation | async-start | bytes 524288 | tf_op jit(solution)/shard_map/cond/branch_0_fun/all_to_all | solution.py:276
  24.8 26.2 %copy-start = (bf16[1024,1024]{1,0:T(8,128)(2,1)S(1)}, bf16[1024,1024]{1,0:T(8,128)(2,1)}, u32[]{:S(2)}) copy-start(bf16[1024,1024]{1,0:T(8,128)(2,1)} %wo_ref.1) | copy-start | bytes 6291460

commit v4 on v3

v4 whole, which is shorter than its diff:
```python
import jax
import jax.numpy as jnp
from jax import lax
from jax.experimental import pallas as pl
from jax.experimental.pallas import tpu as pltpu
from jax.sharding import Mesh
from jax.sharding import PartitionSpec as P

DP = ("dp_0", "dp_1")
VAR = ("y", "core")
F32 = jnp.float32
BF16 = jnp.bfloat16
NT = (((1,), (1,)), ((), ()))
TN = (((0,), (0,)), ((), ()))
PAIRS = [(k, l) for k in range(5) for l in range(k, 5)]


def whole(memory_space=pltpu.VMEM):
    return pl.BlockSpec(memory_space=memory_space)


def iota(shape, dim):
    return lax.broadcasted_iota(jnp.int32, shape, dim)


def picked(hits):
    return jnp.concatenate([jnp.where(hit, 1.0, 0.0) for hit in hits], axis=0).astype(BF16)


def split3(x):
    top = x.astype(BF16).astype(F32)
    mid = (x - top).astype(BF16).astype(F32)
    return top, mid, (x - top - mid).astype(BF16).astype(F32)


def pack_kernel(chip_ref, ids_ref, wk_ref, wv_ref, query_ref, pix_ref, w_ref, send_ref, wk, wv, q_scr, pix, ids, prod, chunk, sems):
    chip = chip_ref[0]
    at = pl.multiple_of(chip * 128, 128)
    copies = [
        pltpu.make_async_copy(ids_ref, ids, sems.at[0]),
        pltpu.make_async_copy(pix_ref, pix, sems.at[1]),
        pltpu.make_async_copy(query_ref, q_scr, sems.at[2]),
        pltpu.make_async_copy(wk_ref.at[:, pl.ds(at, 128)], wk, sems.at[3]),
        pltpu.make_async_copy(wv_ref.at[:, pl.ds(at, 128)], wv, sems.at[4]),
    ]
    for copy in copies:
        copy.start()
    rows = wk.shape[0]
    slots = ids_ref.shape[1]
    prod[...] = jnp.zeros(prod.shape, F32)
    sub, lane = iota((8, 128), 0), iota((8, 128), 1)
    mine = jnp.where(lane // 64 == sub % 2, 1.0, 0.0).astype(BF16)
    for copy in copies[:2]:
        copy.wait()
    own = iota((8, slots), 0) == iota((8, slots), 1)
    meta = jnp.sum(jnp.where(own, ids[...].astype(F32), 0.0), axis=1, keepdims=True)
    meta = jnp.broadcast_to(meta, (8, 128))
    n = 4 * slots
    for half in range(2):
        chunk[32 * half + n : 32 * half + 32, :] = meta
    for s in range(slots):
        x = pix[0, s].astype(F32)
        for half in range(2):
            chunk[32 * half + 4 * s : 32 * half + 4 * s + 4, :] = x[:, 128 * half : 128 * half + 128]
    send_ref[...] = chunk[...].astype(BF16)

    for copy in copies[2:]:
        copy.wait()
    q = q_scr[pl.ds(2 * chip, 2), :]
    prod[0:rows, :] = wk[...].astype(F32) * jnp.concatenate([q[0:1], q[1:2]], axis=1)
    parts = [lax.dot_general(mine, part.astype(BF16), NT, preferred_element_type=F32) for part in split3(prod[...])]
    fold = parts[0] + parts[1] + parts[2]
    top, mid, low = split3(fold)
    part = jnp.where(sub < 2, top, jnp.where(sub < 4, mid, jnp.where(sub < 6, low, 0.0)))
    both = jnp.concatenate([wv[...].astype(F32), part], axis=0).astype(BF16)
    for d in range(w_ref.shape[0]):
        w_ref[d] = both


def table_kernel(pw_ref, ve_ref, gain_ref, bias_ref, hi_ref, lo_ref, gram_ref, ac, af):
    n_pw, width = pw_ref.shape
    n_ve = ve_ref.shape[0]
    total = af.shape[0]
    at = n_pw + 4
    gain = gain_ref[...]

    def centered(x):
        return x - jnp.mean(x, axis=-1, keepdims=True)

    pw = centered(pw_ref[...].astype(F32))
    tiles = width // 128
    for i in range(tiles):
        ac[i, 0:n_pw, :] = pw[:, 128 * i : 128 * i + 128]
    af[0:n_pw, :] = pw * gain
    af[n_pw:at, :] = jnp.zeros((at - n_pw, width), F32)
    ve = centered(ve_ref[...].astype(F32))
    af[at : at + n_ve, :] = ve * gain
    af[at + n_ve : at + n_ve + 1, :] = bias_ref[...]
    af[at + n_ve + 1 : total, :] = jnp.zeros((total - at - n_ve - 1, width), F32)
    a = af[...]
    hi = a.astype(BF16)
    hi_ref[...] = hi
    lo_ref[...] = (a - hi.astype(F32)).astype(BF16)

    sums = [jnp.zeros((n_ve, 128), F32) for _ in PAIRS]
    for i in range(tiles):
        planes = [ac[i, pl.ds(k, n_ve, stride=4), :] for k in range(4)] + [ve[:, 128 * i : 128 * i + 128]]
        sums = [total + planes[k] * planes[l] for total, (k, l) in zip(sums, PAIRS, strict=True)]
    lane = iota((n_ve, 128), 1)
    gram = jnp.zeros((n_ve, 128), F32)
    for i, (k, l) in enumerate(PAIRS):
        g = jnp.sum(sums[i], axis=-1, keepdims=True) * ((1.0 if k == l else 2.0) / width)
        gram = jnp.where(lane == i, g, gram)
    top, mid, low = split3(gram)
    gram = top + pltpu.roll(mid, 16, 1) + pltpu.roll(low, 32, 1)
    gram_ref[...] = jnp.zeros(gram_ref.shape, BF16)
    gram_ref[0:n_ve, :] = gram.astype(BF16)


def slots_kernel(count_ref, got_ref, gram_ref, out_ref):
    n_chip = got_ref.shape[0]
    slots = 12 * n_chip
    x = got_ref[...].reshape(2 * n_chip, 2, 32, 128)
    x = jnp.concatenate([x[:, i].reshape(64 * n_chip, 128) for i in range(2)], axis=1)
    n = iota((slots, x.shape[0]), 0)
    group = (n * 43) >> 8
    within = n - group * 6
    col = iota(n.shape, 1) - group * 32
    hits = [col == within * 4 + k for k in range(4)] + [col == 24 + within]
    moved = jnp.dot(picked(hits), x, preferred_element_type=F32)
    c = [moved[k * slots : (k + 1) * slots] for k in range(4)]
    meta = moved[4 * slots :, :128]
    ids = meta[:, 0:1].astype(jnp.int32)
    n_ve = gram_ref.shape[0]
    gram = jnp.dot(picked([iota((slots, n_ve), 1) == ids]), gram_ref[...], preferred_element_type=F32)
    gram = gram + pltpu.roll(gram, 112, 1) + pltpu.roll(gram, 96, 1)

    def g(k, l):
        i = PAIRS.index((k, l))
        return gram[:, i : i + 1]

    spread = g(4, 4)
    for k in range(4):
        inner = g(k, 4)
        for l in range(k, 4):
            inner = inner + g(k, l) * c[l]
        spread = spread + c[k] * inner
    r = lax.rsqrt(jnp.maximum(spread, 0.0) + 1e-05)
    top = r.astype(BF16)
    planes = [plane.astype(BF16) for plane in c] + [top, (r - top.astype(F32)).astype(BF16)]
    at = 0
    for plane in planes:
        for half in range(2):
            out_ref[at : at + slots, :] = plane[:, 128 * half : 128 * half + 128]
            at += slots
    meta = jnp.where(iota(meta.shape, 1) == 1, count_ref[0].astype(F32), meta)
    out_ref[at : at + slots, :] = meta.astype(BF16)
    at += slots
    out_ref[at:, :] = jnp.zeros((out_ref.shape[0] - at, 128), BF16)


def attend_kernel(core_ref, hi_ref, lo_ref, weights_ref, planes_ref, out_ref, wide, w_scr):
    half = core_ref[0]
    n_dp = weights_ref.shape[1]
    rows = weights_ref.shape[2] - 8
    per = 128 // rows
    for d in range(n_dp):
        wide[d * rows : (d + 1) * rows, 0:128] = weights_ref[0, d, 0:rows, :]
    for i in range(n_dp // per):
        tile = jnp.zeros((8, 128), F32)
        for p in range(per):
            piece = weights_ref[0, i * per + p, rows : rows + 8, :].astype(F32)
            tile = tile + (pltpu.roll(piece, rows * p, 1) if p else piece)
        tile = jnp.concatenate([tile, jnp.zeros((120, 128), F32)], axis=0)
        wide[128 * i : 128 * i + 128, 128:256] = tile.T.astype(BF16)
    w = wide[...]
    t = jnp.dot(hi_ref[...], w, preferred_element_type=F32) + jnp.dot(lo_ref[...], w, preferred_element_type=F32)
    values, keys = t[:, :128], t[:, 128:]
    keys = (keys + pltpu.roll(keys, 126, 1) + pltpu.roll(keys, 124, 1)) * 0.125
    top, mid, low = split3(keys)
    lane = iota(keys.shape, 1)
    parts = jnp.where(lane < 4, pltpu.roll(mid, 2, 1), jnp.where(lane < 6, pltpu.roll(low, 4, 1), 0.0))
    parts = jnp.where(lane < 2, top, parts)
    table = jnp.concatenate([values, parts], axis=1).astype(BF16)

    slots = w_scr.shape[0] // 5
    entries = hi_ref.shape[0]
    at = entries - 96

    def plane(i):
        return jnp.concatenate(
            [planes_ref[1, (2 * i + h) * slots : (2 * i + h + 1) * slots, :].astype(F32) for h in range(2)], axis=1
        )

    meta = planes_ref[1, 12 * slots : 13 * slots, :].astype(F32)
    ids = meta[:, 0:1].astype(jnp.int32)
    col = iota((slots, entries), 1)
    found = jnp.dot(
        picked([col == 4 * ids + k for k in range(4)] + [col == at + ids]), table, preferred_element_type=F32
    )
    lane = iota((5 * slots, 128), 1)
    v = jnp.where(lane // 64 == half, found[:, :128], 0.0).astype(BF16)
    keyed = jnp.sum(jnp.where(lane % 2 == half, found[:, 128:], 0.0), axis=1, keepdims=True)
    one_row = lane[0:1]
    key_bias = jnp.sum(jnp.where(one_row == half, keys[at + 91 : at + 92], 0.0), axis=1, keepdims=True)
    value_bias = jnp.where(one_row // 64 == half, values[at + 91 : at + 92], 0.0)

    c = [plane(k) for k in range(4)]
    r = plane(4) + plane(5)
    dots = keyed[4 * slots :]
    for k in range(4):
        dots = dots + c[k] * keyed[k * slots : (k + 1) * slots]
    scores = r * dots + key_bias
    scores = jnp.where(iota(scores.shape, 0) < meta[:, 1:2].astype(jnp.int32), scores, -1e30)
    peak = jnp.max(scores, axis=0, keepdims=True)
    expo = jnp.exp(scores - peak)
    share = expo * (1.0 / jnp.sum(expo, axis=0, keepdims=True)) * r
    for k in range(4):
        w_scr[k * slots : (k + 1) * slots, :] = (share * c[k]).astype(BF16)
    w_scr[4 * slots :, :] = share.astype(BF16)
    mixed = lax.dot_general(w_scr[...], v, TN, preferred_element_type=F32)
    mixed = mixed + value_bias
    turned = pltpu.roll(mixed, 64, 1)
    first = jnp.where(half == 0, mixed, turned).reshape(-1, 2, 8, 128)
    second = jnp.where(half == 0, turned, mixed).reshape(-1, 2, 8, 128)
    left = iota((first.shape[0], 8, 128), 2) < 64
    out_ref[...] = jnp.where(left, first[:, 0], second[:, 1]).astype(BF16)


def project_out_kernel(m_ref, wo_ref, out_ref):
    left = iota((8, 128), 1) < 64
    parts = []
    for i in range(m_ref.shape[0] // 2):
        a, b = m_ref[2 * i].astype(F32), m_ref[2 * i + 1].astype(F32)
        first = jnp.where(left, a, pltpu.roll(b, 64, 1))
        second = jnp.where(left, pltpu.roll(a, 64, 1), b)
        parts.append(jnp.concatenate([first, second], axis=0))
    mixed = jnp.concatenate(parts, axis=1).astype(BF16)
    out_ref[...] = jnp.dot(mixed, wo_ref[...], preferred_element_type=F32).astype(BF16)


def cost(flops, moved):
    return pl.CostEstimate(flops=flops, transcendentals=0, bytes_accessed=moved)


def on_device(
    pixels,
    var_ids,
    counts,
    patch_weight,
    var_embed,
    norm_gain,
    norm_bias,
    key_weight,
    value_weight,
    query,
    out_weight,
):
    slots, pp, patches = pixels.shape[1:]
    n_var, width = var_embed.shape
    n_dp = lax.axis_size(DP)
    n_chip, n_core = lax.axis_size("y"), lax.axis_size("core")
    n_sv = n_chip * n_core
    all_slots = slots * n_sv
    entries = 464
    rows = key_weight.shape[0] + 8
    smem, vmem = whole(pltpu.SMEM), whole()
    chip = lax.axis_index("y").astype(jnp.int32).reshape(1)
    core = lax.axis_index("core").astype(jnp.int32).reshape(1)

    packed_w, packed_x = pl.pallas_call(
        pack_kernel,
        out_shape=(jax.ShapeDtypeStruct((n_dp, rows, 128), BF16), jax.ShapeDtypeStruct((64, 128), BF16)),
        in_specs=[smem] + [whole(pltpu.HBM)] * 5,
        out_specs=(vmem, vmem),
        scratch_shapes=[
            pltpu.VMEM((rows - 8, 128), BF16),
            pltpu.VMEM((rows - 8, 128), BF16),
            pltpu.VMEM(query.shape, F32),
            pltpu.VMEM(pixels.shape, BF16),
            pltpu.VMEM(var_ids.shape, jnp.int32),
            pltpu.VMEM((128, 128), F32),
            pltpu.VMEM((64, 128), F32),
            pltpu.SemaphoreType.DMA((5,)),
        ],
        name="pack",
    )(chip, var_ids, key_weight, value_weight, query, pixels)
    of_chip = lax.all_gather(packed_x, "core")

    def tables(patch_weight, var_embed, norm_gain, norm_bias):
        return pl.pallas_call(
            table_kernel,
            out_shape=(
                jax.ShapeDtypeStruct((entries, width), BF16),
                jax.ShapeDtypeStruct((entries, width), BF16),
                jax.ShapeDtypeStruct((96, 128), BF16),
            ),
            in_specs=[vmem] * 4,
            out_specs=(vmem,) * 3,
            scratch_shapes=[pltpu.VMEM((width // 128, n_var * pp + 4, 128), F32), pltpu.VMEM((entries, width), F32)],
            cost_estimate=cost(20 * entries * width, 8 * entries * width),
            compiler_params=pltpu.CompilerParams(vmem_limit_bytes=24 << 20),
            name="tables",
        )(
            patch_weight.reshape(n_var * pp, width),
            var_embed,
            norm_gain.reshape(1, width),
            norm_bias.reshape(1, width),
        )

    def weights_of_all(packed_w, of_chip, counts, *params):
        hi, lo, _ = tables(*params)
        return lax.all_to_all(packed_w, DP, 0, 0, tiled=True), hi, lo

    def slots_of_all(packed_w, of_chip, counts, *params):
        hi, lo, gram = tables(*params)
        send = jnp.broadcast_to(of_chip, (n_chip, *of_chip.shape))
        planes = pl.pallas_call(
            slots_kernel,
            out_shape=jax.ShapeDtypeStruct((n_dp * rows, 128), BF16),
            in_specs=[smem, vmem, vmem],
            out_specs=vmem,
            compiler_params=pltpu.CompilerParams(vmem_limit_bytes=24 << 20),
            name="slots",
        )(counts, lax.all_to_all(send, "y", 0, 0, tiled=True), gram)
        return planes.reshape(n_dp, rows, 128), hi, lo

    params = (counts, patch_weight, var_embed, norm_gain, norm_bias)
    mine, hi, lo = lax.cond(core[0] == 0, weights_of_all, slots_of_all, packed_w, of_chip, *params)
    both = lax.all_gather(mine, "core")

    mixed = pl.pallas_call(
        attend_kernel,
        out_shape=jax.ShapeDtypeStruct((n_sv, 8, 128), BF16),
        in_specs=[smem] + [vmem] * 4,
        out_specs=vmem,
        scratch_shapes=[pltpu.VMEM((width, 256), BF16), pltpu.VMEM((5 * all_slots, patches), BF16)],
        compiler_params=pltpu.CompilerParams(vmem_limit_bytes=24 << 20),
        name="attend",
    )(core, hi, lo, both, both.reshape(n_core, n_dp * rows, 128))
    owned = lax.all_to_all(mixed, VAR, 0, 0, tiled=True)

    out = pl.pallas_call(
        project_out_kernel,
        out_shape=jax.ShapeDtypeStruct((patches // n_sv, width), BF16),
        in_specs=[vmem, vmem],
        out_specs=vmem,
        compiler_params=pltpu.CompilerParams(vmem_limit_bytes=16 << 20),
        name="project_out",
    )(owned, out_weight)
    return out[None]


def solution(mesh):
    torus = Mesh(mesh.devices.reshape(4, 8, 8, 2), (*DP, *VAR))
    return jax.shard_map(
        on_device,
        mesh=torus,
        in_specs=(
            P(DP, VAR, None, None),
            P(DP, VAR),
            P(DP),
            P(),
            P(),
            P(),
            P(),
            P(DP, None),
            P(DP, None),
            P(),
            P(),
        ),
        out_specs=P(DP, VAR, None),
        check_vma=False,
    )
```

time: 52.4 us -> 50.3 us (0.960)
  blocking collectives: 31.9 us -> 29.3 us
  Pallas kernels: 6.67 us -> 8.57 us
  local copies, waits for them, and re-layouts: 3.06 us -> 2.31 us
  between operations: 0.67 us -> 0.02 us
    all_gather x1, blocking collectives: 8.19 us -> 6.07 us  [on_device(): both = lax.all_gather(mine, 'core')]
    pallas_call x2 -> x3, Pallas kernels: 4.3 us -> 6.15 us  [the longest x1 2.24 us: slots_of_all(): pl.pallas_call(slots_kernel, out_shape=jax.ShapeDtypeStruct((n_dp * rows,...]
    pad x1 -> x0, local copies, waits for them, and re-layouts: 0.75 us -> none  [pixels_of_all(): jnp.pad(got, ((0, n_dp * rows - got.shape[0]), (0, 0)))]
where the time goes in v4:
time: 50.3 us; the launch traced here: 50 us
  blocking collectives  29.3 us (58%)
  Pallas kernels  8.57 us (17%)
  waiting for transfers between devices  6.28 us (12%)
  starting transfers between devices  3.41 us (7%)
  local copies, waits for them, and re-layouts  2.31 us (5%)
    all_to_all x1, blocking collectives, on_device(): owned = lax.all_to_all(mixed, VAR, 0, 0, tiled=True)  14.7 us
    all_gather x1, blocking collectives, on_device(): of_chip = lax.all_gather(packed_x, 'core')  8.58 us
    all_to_all x1, waiting for transfers between devices, slots_of_all(): lax.all_to_all(send, 'y', 0, 0, tiled=True)  6.28 us
    all_gather x1, blocking collectives, on_device(): both = lax.all_gather(mine, 'core')  6.07 us
    all_to_all x1, starting transfers between devices, slots_of_all(): lax.all_to_all(send, 'y', 0, 0, tiled=True)  3.41 us
    pallas_call x1, Pallas kernels, slots_of_all(): pl.pallas_call(slots_kernel, out_shape=jax.ShapeDtypeStruct((n_dp * rows,...  2.24 us
    pallas_call x1, Pallas kernels, on_device(): pl.pallas_call(attend_kernel, out_shape=jax.ShapeDtypeStruct((n_sv, 8, 12...  2.08 us
    pallas_call x1, Pallas kernels, on_device(): pl.pallas_call(pack_kernel, out_shape=(jax.ShapeDtypeStruct((n_dp, rows,...  1.83 us
  transfers between devices with their start and end apart: 1, of which 1 were waited for; matrix products, arithmetic and copies ran while one was open for 3% of the time, Pallas kernels for 3%

profile of v4, /device:TPU:1, one launch (start us, length us, event | category | flops | bytes accessed | tf_op | source)
XLA Modules:
  0.0 50.0 jit_solution(9000138272126269677)
XLA Ops:
  0.0 1.8 %pack.1 = (bf16[32,40,128]{2,1,0:T(8,128)(2,1)}, bf16[64,128]{1,0:T(8,128)(2,1)}) custom-call(s32[1]{0:T(128)} %bitcast.7.chip_ref, s32[1,6]{1,0:T(1,128)} %ids_ref.1, bf16[32,1024]{1,0:T(8,128)(2,1)} %wk_ref.1, bf16[32,1024]{1,0:T(8,128)(2,1)} %wv_ref.1, f32[16,64]{1,0:T(8,128)} %query_ref.1, bf16[1,6,4,256]{3,2,1,0:T(4,128)(2,1)} %pix_ref.1), custom_call_target="tpu_custom_call" | custom-call | tf_op jit(solution)/shard_map/pack/pallas_call | solution.py:271
  1.8 8.6 %all-gather = bf16[128,128]{1,0:T(8,128)(2,1)S(1)} all-gather(bf16[64,128]{1,0:T(8,128)(2,1)} %get-tuple-element.48), channel_id=2, replica_groups=mesh['dp_0'=4,'dp_1'=8,'y'=8,'core'=2] {'core'}, dimensions={0}, use_global_device_ids=true | all-gather | bytes 49152 | tf_op jit(solution)/shard_map/all_gather | solution.py:288
  10.4 15.7 %conditional.1 = (bf16[32,40,128]{2,1,0:T(8,128)(2,1)}, bf16[464,1024]{1,0:T(8,128)(2,1)S(1)}, bf16[464,1024]{1,0:T(8,128)(2,1)S(1)}) conditional(s32[]{:T(128)} %convert_element_type.3, (bf16[128,128]{1,0:T(8,128)(2,1)S(1)}, bf16[91,4,1024]{2,1,0:T(4,128)(2,1)}, f32[1024]{0:T(1024)}, f32[1024]{0:T(1024)}, bf16[91,1024]{1,0:T(8,128)(2,1)}, ...), branch_computations={%region_0.0_spmd, %region_1.0_spmd} | conditional | flops 9502720 | bytes 7151756 | solution.py:329
  10.4 0.0 copy-start.1
  10.4 0.0 copy-start.3
  10.4 0.0 copy-start.5
  10.4 0.7 %broadcast_in_dim.4 = bf16[8,2,64,128]{3,2,1,0:T(8,128)(2,1)} broadcast(bf16[2,64,128]{2,1,0:T(8,128)(2,1)S(1)} %bitcast.13), dimensions={1,2,3} | broadcast | bytes 294912 | tf_op jit(solution)/shard_map/cond/branch_0_fun/broadcast_in_dim | solution.py:317
  11.2 3.4 %all-to-all-start = ((bf16[8,2,64,128]{3,2,1,0:T(8,128)(2,1)}), bf16[8,2,64,128]{3,2,1,0:T(8,128)(2,1)S(1)}, u32[]{:S(2)}, u32[]{:S(2)}) async-start(bf16[8,2,64,128]{3,2,1,0:T(8,128)(2,1)} %broadcast_in_dim.4), calls=%async_computation | async-start | bytes 524288 | tf_op jit(solution)/shard_map/cond/branch_0_fun/all_to_all | solution.py:325
  14.6 1.5 %reshape.20.pw_ref = bf16[364,1024]{1,0:T(8,128)(2,1)S(1)} reshape(bf16[91,4,1024]{2,1,0:T(4,128)(2,1)} %get-tuple-element.29) | data formatting | bytes 1490944 | tf_op jit(solution)/shard_map/cond/branch_0_fun/reshape | solution.py:305
  16.1 0.0 copy-done.1
  16.2 0.0 copy-done.3
  16.2 0.0 copy-done.5
  16.2 1.4 %tables.2 = (bf16[464,1024]{1,0:T(8,128)(2,1)S(1)}, bf16[464,1024]{1,0:T(8,128)(2,1)S(1)}, bf16[96,128]{1,0:T(8,128)(2,1)S(1)}) custom-call(bf16[364,1024]{1,0:T(8,128)(2,1)S(1)} %reshape.20.pw_ref, bf16[91,1024]{1,0:T(8,128)(2,1)S(1)} %copy-done.1, f32[1,1024]{1,0:T(1,128)S(1)} %bitcast.14, f32[1,1024]{1,0:T(1,128)S(1)} %bitcast.16), custom_call_target="tpu_custom_call" | custom-call | flops 9502720 | bytes 3801088 | tf_op jit(solution)/shard_map/cond/branch_0_fun/tables/pallas_call | solution.py:291
  17.6 6.3 %all-to-all-done.got_ref = bf16[8,2,64,128]{3,2,1,0:T(8,128)(2,1)S(1)} async-done(((bf16[8,2,64,128]{3,2,1,0:T(8,128)(2,1)}), bf16[8,2,64,128]{3,2,1,0:T(8,128)(2,1)S(1)}, u32[]{:S(2)}, u32[]{:S(2)}) %all-to-all-start) | async-done | bytes 262176 | tf_op jit(solution)/shard_map/cond/branch_0_fun/all_to_all | solution.py:325
  23.8 2.2 %slots.1 = bf16[1280,128]{1,0:T(8,128)(2,1)} custom-call(s32[1]{0:T(128)} %get-tuple-element.54.count_ref, bf16[8,2,64,128]{3,2,1,0:T(8,128)(2,1)S(1)} %all-to-all-done.got_ref, bf16[96,128]{1,0:T(8,128)(2,1)S(1)} %get-tuple-element.33.gram_ref), custom_call_target="tpu_custom_call" | custom-call | tf_op jit(solution)/shard_map/cond/branch_0_fun/slots/pallas_call | solution.py:318
  26.1 0.0 copy-start
  26.1 6.1 %all-gather.1 = bf16[64,40,128]{2,1,0:T(8,128)(2,1)S(1)} all-gather(bf16[32,40,128]{2,1,0:T(8,128)(2,1)} %get-tuple-element.52), channel_id=3, replica_groups=mesh['dp_0'=4,'dp_1'=8,'y'=8,'core'=2] {'core'}, dimensions={0}, use_global_device_ids=true | all-gather | bytes 983040 | tf_op jit(solution)/shard_map/all_gather | solution.py:330
  32.2 2.1 %attend.1 = bf16[16,8,128]{2,1,0:T(8,128)(2,1)S(1)} custom-call(s32[1]{0:T(128)} %bitcast.6.core_ref, bf16[464,1024]{1,0:T(8,128)(2,1)S(1)} %get-tuple-element.50.hi_ref, bf16[464,1024]{1,0:T(8,128)(2,1)S(1)} %get-tuple-element.51.lo_ref, bf16[2,32,40,128]{3,2,1,0:T(8,128)(2,1)S(1)} %bitcast.11, bf16[2,1280,128]{2,1,0:T(8,128)(2,1)S(1)} %bitcast.12), custom_call_target="tpu_custom_call" | custom-call | tf_op jit(solution)/shard_map/attend/pallas_call | solution.py:332
  34.2 14.7 %all_to_all.13.m_ref = bf16[16,8,128]{2,1,0:T(8,128)(2,1)S(1)} all-to-all(bf16[16,8,128]{2,1,0:T(8,128)(2,1)S(1)} %attend.1), channel_id=1, replica_groups=mesh['dp_0'=4,'dp_1'=8,'y'=8,'core'=2] {'y','core'}, dimensions={0} | all-to-all | bytes 65536 | tf_op jit(solution)/shard_map/all_to_all | solution.py:341
  48.9 0.0 copy-done
  48.9 1.0 %project_out.1 = bf16[16,1024]{1,0:T(8,128)(2,1)} custom-call(bf16[16,8,128]{2,1,0:T(8,128)(2,1)S(1)} %all_to_all.13.m_ref, bf16[1024,1024]{1,0:T(8,128)(2,1)S(1)} %copy-done), custom_call_target="tpu_custom_call" | custom-call | tf_op jit(solution)/shard_map/project_out/pallas_call | solution.py:343
Async XLA Ops:
  10.4 5.7 %copy-start.1 = (bf16[91,1024]{1,0:T(8,128)(2,1)S(1)}, bf16[91,1024]{1,0:T(8,128)(2,1)}, u32[]{:S(2)}) copy-start(bf16[91,1024]{1,0:T(8,128)(2,1)} %get-tuple-element.30.ve_ref) | copy-start | bytes 559108 | tf_op jit(solution)/shard_map/cond
  10.4 5.7 %copy-start.3 = (f32[1024]{0:T(1024)S(1)}, f32[1024]{0:T(1024)}, u32[]{:S(2)}) copy-start(f32[1024]{0:T(1024)} %get-tuple-element.31) | copy-start | bytes 12292 | tf_op jit(solution)/shard_map/cond
  10.4 5.7 %copy-start.5 = (f32[1024]{0:T(1024)S(1)}, f32[1024]{0:T(1024)}, u32[]{:S(2)}) copy-start(f32[1024]{0:T(1024)} %get-tuple-element.32) | copy-start | bytes 12292 | tf_op jit(solution)/shard_map/cond
  11.2 12.7 %all-to-all-start = ((bf16[8,2,64,128]{3,2,1,0:T(8,128)(2,1)}), bf16[8,2,64,128]{3,2,1,0:T(8,128)(2,1)S(1)}, u32[]{:S(2)}, u32[]{:S(2)}) async-start(bf16[8,2,64,128]{3,2,1,0:T(8,128)(2,1)} %broadcast_in_dim.4), calls=%async_computation | async-start | bytes 524288 | tf_op jit(solution)/shard_map/cond/branch_0_fun/all_to_all | solution.py:325
  26.1 22.8 %copy-start = (bf16[1024,1024]{1,0:T(8,128)(2,1)S(1)}, bf16[1024,1024]{1,0:T(8,128)(2,1)}, u32[]{:S(2)}) copy-start(bf16[1024,1024]{1,0:T(8,128)(2,1)} %wo_ref.1) | copy-start | bytes 6291460

commit v5 on v4

--- a/solution.py
+++ b/solution.py
@@ -33,8 +33,8 @@
     return top, mid, (x - top - mid).astype(BF16).astype(F32)
 
 
-def pack_kernel(chip_ref, ids_ref, wk_ref, wv_ref, query_ref, pix_ref, w_ref, send_ref, wk, wv, q_scr, pix, ids, prod, chunk, sems):
-    chip = chip_ref[0]
+def pack_kernel(ids_ref, wk_ref, wv_ref, query_ref, pix_ref, w_ref, send_ref, wk, wv, q_scr, pix, ids, prod, chunk, sems):
+    chip = lax.axis_index("y")
     at = pl.multiple_of(chip * 128, 128)
     copies = [
         pltpu.make_async_copy(ids_ref, ids, sems.at[0]),
@@ -77,10 +77,10 @@
         w_ref[d] = both
 
 
-def table_kernel(pw_ref, ve_ref, gain_ref, bias_ref, hi_ref, lo_ref, gram_ref, ac, af):
+def table_kernel(pw_ref, ve_ref, gain_ref, bias_ref, rows_ref, gram_ref, ac):
     n_pw, width = pw_ref.shape
     n_ve = ve_ref.shape[0]
-    total = af.shape[0]
+    total = rows_ref.shape[0]
     at = n_pw + 4
     gain = gain_ref[...]
 
@@ -91,16 +91,11 @@
     tiles = width // 128
     for i in range(tiles):
         ac[i, 0:n_pw, :] = pw[:, 128 * i : 128 * i + 128]
-    af[0:n_pw, :] = pw * gain
-    af[n_pw:at, :] = jnp.zeros((at - n_pw, width), F32)
     ve = centered(ve_ref[...].astype(F32))
-    af[at : at + n_ve, :] = ve * gain
-    af[at + n_ve : at + n_ve + 1, :] = bias_ref[...]
-    af[at + n_ve + 1 : total, :] = jnp.zeros((total - at - n_ve - 1, width), F32)
-    a = af[...]
-    hi = a.astype(BF16)
-    hi_ref[...] = hi
-    lo_ref[...] = (a - hi.astype(F32)).astype(BF16)
+    pw = jnp.concatenate([pw * gain, jnp.zeros((at - n_pw, width), F32)], axis=0)
+    rows_ref[0:at, :] = pw.astype(BF16)
+    rest = jnp.zeros((total - at - n_ve - 1, width), F32)
+    rows_ref[at:, :] = jnp.concatenate([ve * gain, bias_ref[...], rest], axis=0).astype(BF16)
 
     sums = [jnp.zeros((n_ve, 128), F32) for _ in PAIRS]
     for i in range(tiles):
@@ -159,8 +154,8 @@
     out_ref[at:, :] = jnp.zeros((out_ref.shape[0] - at, 128), BF16)
 
 
-def attend_kernel(core_ref, hi_ref, lo_ref, weights_ref, planes_ref, out_ref, wide, w_scr):
-    half = core_ref[0]
+def attend_kernel(rows_ref, weights_ref, planes_ref, out_ref, wide, w_scr):
+    half = lax.axis_index("core")
     n_dp = weights_ref.shape[1]
     rows = weights_ref.shape[2] - 8
     per = 128 // rows
@@ -174,17 +169,14 @@
         tile = jnp.concatenate([tile, jnp.zeros((120, 128), F32)], axis=0)
         wide[128 * i : 128 * i + 128, 128:256] = tile.T.astype(BF16)
     w = wide[...]
-    t = jnp.dot(hi_ref[...], w, preferred_element_type=F32) + jnp.dot(lo_ref[...], w, preferred_element_type=F32)
+    t = jnp.dot(rows_ref[...], w, preferred_element_type=F32)
     values, keys = t[:, :128], t[:, 128:]
-    keys = (keys + pltpu.roll(keys, 126, 1) + pltpu.roll(keys, 124, 1)) * 0.125
     top, mid, low = split3(keys)
-    lane = iota(keys.shape, 1)
-    parts = jnp.where(lane < 4, pltpu.roll(mid, 2, 1), jnp.where(lane < 6, pltpu.roll(low, 4, 1), 0.0))
-    parts = jnp.where(lane < 2, top, parts)
+    parts = top + pltpu.roll(mid, 8, 1) + pltpu.roll(low, 16, 1)
     table = jnp.concatenate([values, parts], axis=1).astype(BF16)
 
     slots = w_scr.shape[0] // 5
-    entries = hi_ref.shape[0]
+    entries = rows_ref.shape[0]
     at = entries - 96
 
     def plane(i):
@@ -198,12 +190,13 @@
     found = jnp.dot(
         picked([col == 4 * ids + k for k in range(4)] + [col == at + ids]), table, preferred_element_type=F32
     )
-    lane = iota((5 * slots, 128), 1)
-    v = jnp.where(lane // 64 == half, found[:, :128], 0.0).astype(BF16)
-    keyed = jnp.sum(jnp.where(lane % 2 == half, found[:, 128:], 0.0), axis=1, keepdims=True)
-    one_row = lane[0:1]
-    key_bias = jnp.sum(jnp.where(one_row == half, keys[at + 91 : at + 92], 0.0), axis=1, keepdims=True)
-    value_bias = jnp.where(one_row // 64 == half, values[at + 91 : at + 92], 0.0)
+    lane = iota((1, 128), 1)
+    key_lanes = jnp.where(lane % 2 == half, 0.125, 0.0)
+    value_lanes = jnp.where(lane // 64 == half, 1.0, 0.0)
+    v = (found[:, :128] * value_lanes).astype(BF16)
+    keyed = jnp.sum(found[:, 128:] * key_lanes, axis=1, keepdims=True)
+    key_bias = jnp.sum(keys[at + 91 : at + 92] * key_lanes, axis=1, keepdims=True)
+    value_bias = values[at + 91 : at + 92] * value_lanes
 
     c = [plane(k) for k in range(4)]
     r = plane(4) + plane(5)
@@ -218,7 +211,7 @@
     for k in range(4):
         w_scr[k * slots : (k + 1) * slots, :] = (share * c[k]).astype(BF16)
     w_scr[4 * slots :, :] = share.astype(BF16)
-    mixed = lax.dot_general(w_scr[...], v, TN, preferred_element_type=F32)
+    mixed = lax.dot_general(v, w_scr[...], TN, preferred_element_type=F32).T
     mixed = mixed + value_bias
     turned = pltpu.roll(mixed, 64, 1)
     first = jnp.where(half == 0, mixed, turned).reshape(-1, 2, 8, 128)
@@ -265,13 +258,11 @@
     entries = 464
     rows = key_weight.shape[0] + 8
     smem, vmem = whole(pltpu.SMEM), whole()
-    chip = lax.axis_index("y").astype(jnp.int32).reshape(1)
-    core = lax.axis_index("core").astype(jnp.int32).reshape(1)
 
     packed_w, packed_x = pl.pallas_call(
         pack_kernel,
         out_shape=(jax.ShapeDtypeStruct((n_dp, rows, 128), BF16), jax.ShapeDtypeStruct((64, 128), BF16)),
-        in_specs=[smem] + [whole(pltpu.HBM)] * 5,
+        in_specs=[whole(pltpu.HBM)] * 5,
         out_specs=(vmem, vmem),
         scratch_shapes=[
             pltpu.VMEM((rows - 8, 128), BF16),
@@ -284,7 +275,7 @@
             pltpu.SemaphoreType.DMA((5,)),
         ],
         name="pack",
-    )(chip, var_ids, key_weight, value_weight, query, pixels)
+    )(var_ids, key_weight, value_weight, query, pixels)
     of_chip = lax.all_gather(packed_x, "core")
 
     def tables(patch_weight, var_embed, norm_gain, norm_bias):
@@ -292,12 +283,11 @@
             table_kernel,
             out_shape=(
                 jax.ShapeDtypeStruct((entries, width), BF16),
-                jax.ShapeDtypeStruct((entries, width), BF16),
                 jax.ShapeDtypeStruct((96, 128), BF16),
             ),
             in_specs=[vmem] * 4,
-            out_specs=(vmem,) * 3,
-            scratch_shapes=[pltpu.VMEM((width // 128, n_var * pp + 4, 128), F32), pltpu.VMEM((entries, width), F32)],
+            out_specs=(vmem,) * 2,
+            scratch_shapes=[pltpu.VMEM((width // 128, n_var * pp + 4, 128), F32)],
             cost_estimate=cost(20 * entries * width, 8 * entries * width),
             compiler_params=pltpu.CompilerParams(vmem_limit_bytes=24 << 20),
             name="tables",
@@ -309,11 +299,11 @@
         )
 
     def weights_of_all(packed_w, of_chip, counts, *params):
-        hi, lo, _ = tables(*params)
-        return lax.all_to_all(packed_w, DP, 0, 0, tiled=True), hi, lo
+        table, _ = tables(*params)
+        return lax.all_to_all(packed_w, DP, 0, 0, tiled=True), table
 
     def slots_of_all(packed_w, of_chip, counts, *params):
-        hi, lo, gram = tables(*params)
+        table, gram = tables(*params)
         send = jnp.broadcast_to(of_chip, (n_chip, *of_chip.shape))
         planes = pl.pallas_call(
             slots_kernel,
@@ -323,21 +313,21 @@
             compiler_params=pltpu.CompilerParams(vmem_limit_bytes=24 << 20),
             name="slots",
         )(counts, lax.all_to_all(send, "y", 0, 0, tiled=True), gram)
-        return planes.reshape(n_dp, rows, 128), hi, lo
+        return planes.reshape(n_dp, rows, 128), table
 
     params = (counts, patch_weight, var_embed, norm_gain, norm_bias)
-    mine, hi, lo = lax.cond(core[0] == 0, weights_of_all, slots_of_all, packed_w, of_chip, *params)
+    mine, table = lax.cond(lax.axis_index("core") == 0, weights_of_all, slots_of_all, packed_w, of_chip, *params)
     both = lax.all_gather(mine, "core")
 
     mixed = pl.pallas_call(
         attend_kernel,
         out_shape=jax.ShapeDtypeStruct((n_sv, 8, 128), BF16),
-        in_specs=[smem] + [vmem] * 4,
+        in_specs=[vmem] * 3,
         out_specs=vmem,
         scratch_shapes=[pltpu.VMEM((width, 256), BF16), pltpu.VMEM((5 * all_slots, patches), BF16)],
         compiler_params=pltpu.CompilerParams(vmem_limit_bytes=24 << 20),
         name="attend",
-    )(core, hi, lo, both, both.reshape(n_core, n_dp * rows, 128))
+    )(table, both, both.reshape(n_core, n_dp * rows, 128))
     owned = lax.all_to_all(mixed, VAR, 0, 0, tiled=True)
 
     out = pl.pallas_call(

time: 50.3 us -> 49.9 us (level)
  Pallas kernels: 8.57 us -> 7.98 us
  transfers between devices with their start and end apart: 1 -> 1, of which waited for: 1 -> 1; matrix products, arithmetic and copies ran while one was open for 3% -> 3% of each run, Pallas kernels for 3% -> 2%
where the time goes in v5:
time: 49.9 us; the launch traced here: 49.6 us
  blocking collectives  29.3 us (59%)
  Pallas kernels  7.98 us (16%)
  waiting for transfers between devices  6.47 us (13%)
  starting transfers between devices  3.41 us (7%)
  local copies, waits for them, and re-layouts  2.31 us (5%)
    all_to_all x1, blocking collectives, on_device(): owned = lax.all_to_all(mixed, VAR, 0, 0, tiled=True)  14.7 us
    all_gather x1, blocking collectives, on_device(): of_chip = lax.all_gather(packed_x, 'core')  8.58 us
    all_to_all x1, waiting for transfers between devices, slots_of_all(): lax.all_to_all(send, 'y', 0, 0, tiled=True)  6.47 us
    all_gather x1, blocking collectives, on_device(): both = lax.all_gather(mine, 'core')  6.07 us
    all_to_all x1, starting transfers between devices, slots_of_all(): lax.all_to_all(send, 'y', 0, 0, tiled=True)  3.41 us
    pallas_call x1, Pallas kernels, slots_of_all(): pl.pallas_call(slots_kernel, out_shape=jax.ShapeDtypeStruct((n_dp * rows,...  2.24 us
    pallas_call x1, Pallas kernels, on_device(): pl.pallas_call(pack_kernel, out_shape=(jax.ShapeDtypeStruct((n_dp, rows,...  1.83 us
    pallas_call x1, Pallas kernels, on_device(): pl.pallas_call(attend_kernel, out_shape=jax.ShapeDtypeStruct((n_sv, 8, 12...  1.68 us
  transfers between devices with their start and end apart: 1, of which 1 were waited for; matrix products, arithmetic and copies ran while one was open for 3% of the time, Pallas kernels for 2%

profile of v5, /device:TPU:1, one launch (start us, length us, event | category | flops | bytes accessed | tf_op | source)
XLA Modules:
  0.0 49.6 jit_solution(7545477657879237757)
XLA Ops:
  0.0 1.8 %pack.1 = (bf16[32,40,128]{2,1,0:T(8,128)(2,1)}, bf16[64,128]{1,0:T(8,128)(2,1)}) custom-call(s32[1,6]{1,0:T(1,128)} %ids_ref.1, bf16[32,1024]{1,0:T(8,128)(2,1)} %wk_ref.1, bf16[32,1024]{1,0:T(8,128)(2,1)} %wv_ref.1, f32[16,64]{1,0:T(8,128)} %query_ref.1, bf16[1,6,4,256]{3,2,1,0:T(4,128)(2,1)} %pix_ref.1), custom_call_target="tpu_custom_call" | custom-call | tf_op jit(solution)/shard_map/pack/pallas_call | solution.py:262
  1.8 8.6 %all-gather = bf16[128,128]{1,0:T(8,128)(2,1)S(1)} all-gather(bf16[64,128]{1,0:T(8,128)(2,1)} %get-tuple-element.45), channel_id=2, replica_groups=mesh['dp_0'=4,'dp_1'=8,'y'=8,'core'=2] {'core'}, dimensions={0}, use_global_device_ids=true | all-gather | bytes 49152 | tf_op jit(solution)/shard_map/all_gather | solution.py:279
  10.4 15.7 %conditional.1 = (bf16[32,40,128]{2,1,0:T(8,128)(2,1)}, bf16[464,1024]{1,0:T(8,128)(2,1)S(1)}) conditional(s32[]{:T(128)} %convert_element_type.3, (bf16[128,128]{1,0:T(8,128)(2,1)S(1)}, bf16[91,4,1024]{2,1,0:T(4,128)(2,1)}, f32[1024]{0:T(1024)}, f32[1024]{0:T(1024)}, bf16[91,1024]{1,0:T(8,128)(2,1)}, /*index=5*/s32[1]{0:T(128)}) %tuple.13, ...), branch_computations={%region_0.0_spmd, %region_1.0_spmd} | conditional | flops 9502720 | bytes 7151748 | solution.py:319
  10.4 0.0 copy-start.1
  10.4 0.0 copy-start.3
  10.4 0.0 copy-start.5
  10.4 0.7 %broadcast_in_dim.4 = bf16[8,2,64,128]{3,2,1,0:T(8,128)(2,1)} broadcast(bf16[2,64,128]{2,1,0:T(8,128)(2,1)S(1)} %bitcast.11), dimensions={1,2,3} | broadcast | bytes 294912 | tf_op jit(solution)/shard_map/cond/branch_0_fun/broadcast_in_dim | solution.py:307
  11.2 3.4 %all-to-all-start = ((bf16[8,2,64,128]{3,2,1,0:T(8,128)(2,1)}), bf16[8,2,64,128]{3,2,1,0:T(8,128)(2,1)S(1)}, u32[]{:S(2)}, u32[]{:S(2)}) async-start(bf16[8,2,64,128]{3,2,1,0:T(8,128)(2,1)} %broadcast_in_dim.4), calls=%async_computation | async-start | bytes 524288 | tf_op jit(solution)/shard_map/cond/branch_0_fun/all_to_all | solution.py:315
  14.6 1.5 %reshape.16.pw_ref = bf16[364,1024]{1,0:T(8,128)(2,1)S(1)} reshape(bf16[91,4,1024]{2,1,0:T(4,128)(2,1)} %get-tuple-element.29) | data formatting | bytes 1490944 | tf_op jit(solution)/shard_map/cond/branch_0_fun/reshape | solution.py:295
  16.1 0.0 copy-done.1
  16.2 0.0 copy-done.3
  16.2 0.0 copy-done.5
  16.2 1.2 %tables.2 = (bf16[464,1024]{1,0:T(8,128)(2,1)S(1)}, bf16[96,128]{1,0:T(8,128)(2,1)S(1)}) custom-call(bf16[364,1024]{1,0:T(8,128)(2,1)S(1)} %reshape.16.pw_ref, bf16[91,1024]{1,0:T(8,128)(2,1)S(1)} %copy-done.1, f32[1,1024]{1,0:T(1,128)S(1)} %bitcast.12, f32[1,1024]{1,0:T(1,128)S(1)} %bitcast.14), custom_call_target="tpu_custom_call" | custom-call | flops 9502720 | bytes 3801088 | tf_op jit(solution)/shard_map/cond/branch_0_fun/tables/pallas_call | solution.py:282
  17.4 6.5 %all-to-all-done.got_ref = bf16[8,2,64,128]{3,2,1,0:T(8,128)(2,1)S(1)} async-done(((bf16[8,2,64,128]{3,2,1,0:T(8,128)(2,1)}), bf16[8,2,64,128]{3,2,1,0:T(8,128)(2,1)S(1)}, u32[]{:S(2)}, u32[]{:S(2)}) %all-to-all-start) | async-done | bytes 262176 | tf_op jit(solution)/shard_map/cond/branch_0_fun/all_to_all | solution.py:315
  23.8 2.2 %slots.1 = bf16[1280,128]{1,0:T(8,128)(2,1)} custom-call(s32[1]{0:T(128)} %get-tuple-element.50.count_ref, bf16[8,2,64,128]{3,2,1,0:T(8,128)(2,1)S(1)} %all-to-all-done.got_ref, bf16[96,128]{1,0:T(8,128)(2,1)S(1)} %get-tuple-element.33.gram_ref), custom_call_target="tpu_custom_call" | custom-call | tf_op jit(solution)/shard_map/cond/branch_0_fun/slots/pallas_call | solution.py:308
  26.1 0.0 copy-start
  26.1 6.1 %all-gather.1 = bf16[64,40,128]{2,1,0:T(8,128)(2,1)S(1)} all-gather(bf16[32,40,128]{2,1,0:T(8,128)(2,1)} %get-tuple-element.48), channel_id=3, replica_groups=mesh['dp_0'=4,'dp_1'=8,'y'=8,'core'=2] {'core'}, dimensions={0}, use_global_device_ids=true | all-gather | bytes 983040 | tf_op jit(solution)/shard_map/all_gather | solution.py:320
  32.2 1.7 %attend.1 = bf16[16,8,128]{2,1,0:T(8,128)(2,1)S(1)} custom-call(bf16[464,1024]{1,0:T(8,128)(2,1)S(1)} %get-tuple-element.47.rows_ref, bf16[2,32,40,128]{3,2,1,0:T(8,128)(2,1)S(1)} %bitcast.9, bf16[2,1280,128]{2,1,0:T(8,128)(2,1)S(1)} %bitcast.10), custom_call_target="tpu_custom_call" | custom-call | tf_op jit(solution)/shard_map/attend/pallas_call | solution.py:322
  33.8 14.7 %all_to_all.13.m_ref = bf16[16,8,128]{2,1,0:T(8,128)(2,1)S(1)} all-to-all(bf16[16,8,128]{2,1,0:T(8,128)(2,1)S(1)} %attend.1), channel_id=1, replica_groups=mesh['dp_0'=4,'dp_1'=8,'y'=8,'core'=2] {'y','core'}, dimensions={0} | all-to-all | bytes 65536 | tf_op jit(solution)/shard_map/all_to_all | solution.py:331
  48.5 0.0 copy-done
  48.5 1.0 %project_out.1 = bf16[16,1024]{1,0:T(8,128)(2,1)} custom-call(bf16[16,8,128]{2,1,0:T(8,128)(2,1)S(1)} %all_to_all.13.m_ref, bf16[1024,1024]{1,0:T(8,128)(2,1)S(1)} %copy-done), custom_call_target="tpu_custom_call" | custom-call | tf_op jit(solution)/shard_map/project_out/pallas_call | solution.py:333
Async XLA Ops:
  10.4 5.7 %copy-start.1 = (bf16[91,1024]{1,0:T(8,128)(2,1)S(1)}, bf16[91,1024]{1,0:T(8,128)(2,1)}, u32[]{:S(2)}) copy-start(bf16[91,1024]{1,0:T(8,128)(2,1)} %get-tuple-element.30.ve_ref) | copy-start | bytes 559108 | tf_op jit(solution)/shard_map/cond
  10.4 5.7 %copy-start.3 = (f32[1024]{0:T(1024)S(1)}, f32[1024]{0:T(1024)}, u32[]{:S(2)}) copy-start(f32[1024]{0:T(1024)} %get-tuple-element.31) | copy-start | bytes 12292 | tf_op jit(solution)/shard_map/cond
  10.4 5.7 %copy-start.5 = (f32[1024]{0:T(1024)S(1)}, f32[1024]{0:T(1024)}, u32[]{:S(2)}) copy-start(f32[1024]{0:T(1024)} %get-tuple-element.32) | copy-start | bytes 12292 | tf_op jit(solution)/shard_map/cond
  11.2 12.7 %all-to-all-start = ((bf16[8,2,64,128]{3,2,1,0:T(8,128)(2,1)}), bf16[8,2,64,128]{3,2,1,0:T(8,128)(2,1)S(1)}, u32[]{:S(2)}, u32[]{:S(2)}) async-start(bf16[8,2,64,128]{3,2,1,0:T(8,128)(2,1)} %broadcast_in_dim.4), calls=%async_computation | async-start | bytes 524288 | tf_op jit(solution)/shard_map/cond/branch_0_fun/all_to_all | solution.py:315
  26.1 22.4 %copy-start = (bf16[1024,1024]{1,0:T(8,128)(2,1)S(1)}, bf16[1024,1024]{1,0:T(8,128)(2,1)}, u32[]{:S(2)}) copy-start(bf16[1024,1024]{1,0:T(8,128)(2,1)} %wo_ref.1) | copy-start | bytes 6291460

commit v6 on v5

--- a/solution.py
+++ b/solution.py
@@ -33,7 +33,7 @@
     return top, mid, (x - top - mid).astype(BF16).astype(F32)
 
 
-def pack_kernel(ids_ref, wk_ref, wv_ref, query_ref, pix_ref, w_ref, send_ref, wk, wv, q_scr, pix, ids, prod, chunk, sems):
+def pack_kernel(ids_ref, wk_ref, wv_ref, query_ref, pix_ref, w_ref, send_ref, wk, wv, q_scr, pix, ids, prod, chunk, stage, sems):
     chip = lax.axis_index("y")
     at = pl.multiple_of(chip * 128, 128)
     copies = [
@@ -50,6 +50,25 @@
     prod[...] = jnp.zeros(prod.shape, F32)
     sub, lane = iota((8, 128), 0), iota((8, 128), 1)
     mine = jnp.where(lane // 64 == sub % 2, 1.0, 0.0).astype(BF16)
+    for copy in copies[2:]:
+        copy.wait()
+    q = q_scr[pl.ds(2 * chip, 2), :]
+    prod[0:rows, :] = wk[...].astype(F32) * jnp.concatenate([q[0:1], q[1:2]], axis=1)
+    parts = [lax.dot_general(mine, part.astype(BF16), NT, preferred_element_type=F32) for part in split3(prod[...])]
+    fold = parts[0] + parts[1] + parts[2]
+    top, mid, low = split3(fold)
+    part = jnp.where(sub < 2, top, jnp.where(sub < 4, mid, jnp.where(sub < 6, low, 0.0)))
+    both = jnp.concatenate([wv[...].astype(F32), part], axis=0).astype(BF16)
+    each = stage.shape[0]
+    for d in range(each):
+        stage[d] = both
+    sends = [
+        pltpu.make_async_copy(stage, w_ref.at[pl.ds(each * i, each)], sems.at[5 + i])
+        for i in range(w_ref.shape[0] // each)
+    ]
+    for send in sends:
+        send.start()
+
     for copy in copies[:2]:
         copy.wait()
     own = iota((8, slots), 0) == iota((8, slots), 1)
@@ -63,18 +82,8 @@
         for half in range(2):
             chunk[32 * half + 4 * s : 32 * half + 4 * s + 4, :] = x[:, 128 * half : 128 * half + 128]
     send_ref[...] = chunk[...].astype(BF16)
-
-    for copy in copies[2:]:
-        copy.wait()
-    q = q_scr[pl.ds(2 * chip, 2), :]
-    prod[0:rows, :] = wk[...].astype(F32) * jnp.concatenate([q[0:1], q[1:2]], axis=1)
-    parts = [lax.dot_general(mine, part.astype(BF16), NT, preferred_element_type=F32) for part in split3(prod[...])]
-    fold = parts[0] + parts[1] + parts[2]
-    top, mid, low = split3(fold)
-    part = jnp.where(sub < 2, top, jnp.where(sub < 4, mid, jnp.where(sub < 6, low, 0.0)))
-    both = jnp.concatenate([wv[...].astype(F32), part], axis=0).astype(BF16)
-    for d in range(w_ref.shape[0]):
-        w_ref[d] = both
+    for send in sends:
+        send.wait()
 
 
 def table_kernel(pw_ref, ve_ref, gain_ref, bias_ref, rows_ref, gram_ref, ac):
@@ -261,9 +270,9 @@
 
     packed_w, packed_x = pl.pallas_call(
         pack_kernel,
-        out_shape=(jax.ShapeDtypeStruct((n_dp, rows, 128), BF16), jax.ShapeDtypeStruct((64, 128), BF16)),
+        out_shape=(jax.ShapeDtypeStruct((n_dp, rows, 128), BF16), pltpu.VMEM((64, 128), BF16)),
         in_specs=[whole(pltpu.HBM)] * 5,
-        out_specs=(vmem, vmem),
+        out_specs=(whole(pltpu.HBM), vmem),
         scratch_shapes=[
             pltpu.VMEM((rows - 8, 128), BF16),
             pltpu.VMEM((rows - 8, 128), BF16),
@@ -272,7 +281,8 @@
             pltpu.VMEM(var_ids.shape, jnp.int32),
             pltpu.VMEM((128, 128), F32),
             pltpu.VMEM((64, 128), F32),
-            pltpu.SemaphoreType.DMA((5,)),
+            pltpu.VMEM((n_dp // 4, rows, 128), BF16),
+            pltpu.SemaphoreType.DMA((9,)),
         ],
         name="pack",
     )(var_ids, key_weight, value_weight, query, pixels)

time: 49.9 us -> 49.6 us (level)
  no operation moved by 1% of the time
where the time goes in v6:
time: 49.6 us; the launch traced here: 49.3 us
  blocking collectives  29.1 us (59%)
  Pallas kernels  7.96 us (16%)
  waiting for transfers between devices  6.47 us (13%)
  starting transfers between devices  3.41 us (7%)
  local copies, waits for them, and re-layouts  2.3 us (5%)
    all_to_all x1, blocking collectives, on_device(): owned = lax.all_to_all(mixed, VAR, 0, 0, tiled=True)  14.7 us
    all_gather x1, blocking collectives, on_device(): of_chip = lax.all_gather(packed_x, 'core')  8.37 us
    all_to_all x1, waiting for transfers between devices, slots_of_all(): lax.all_to_all(send, 'y', 0, 0, tiled=True)  6.47 us
    all_gather x1, blocking collectives, on_device(): both = lax.all_gather(mine, 'core')  6.07 us
    all_to_all x1, starting transfers between devices, slots_of_all(): lax.all_to_all(send, 'y', 0, 0, tiled=True)  3.41 us
    pallas_call x1, Pallas kernels, slots_of_all(): pl.pallas_call(slots_kernel, out_shape=jax.ShapeDtypeStruct((n_dp * rows,...  2.24 us
    pallas_call x1, Pallas kernels, on_device(): pl.pallas_call(pack_kernel, out_shape=(jax.ShapeDtypeStruct((n_dp, rows,...  1.81 us
    pallas_call x1, Pallas kernels, on_device(): pl.pallas_call(attend_kernel, out_shape=jax.ShapeDtypeStruct((n_sv, 8, 12...  1.68 us
  transfers between devices with their start and end apart: 1, of which 1 were waited for; matrix products, arithmetic and copies ran while one was open for 3% of the time, Pallas kernels for 2%

profile of v6, /device:TPU:1, one launch (start us, length us, event | category | flops | bytes accessed | tf_op | source)
XLA Modules:
  0.0 49.3 jit_solution(18043259065356161377)
XLA Ops:
  0.0 1.8 %pack.1 = (bf16[32,40,128]{2,1,0:T(8,128)(2,1)}, bf16[64,128]{1,0:T(8,128)(2,1)S(1)}) custom-call(s32[1,6]{1,0:T(1,128)} %ids_ref.1, bf16[32,1024]{1,0:T(8,128)(2,1)} %wk_ref.1, bf16[32,1024]{1,0:T(8,128)(2,1)} %wv_ref.1, f32[16,64]{1,0:T(8,128)} %query_ref.1, bf16[1,6,4,256]{3,2,1,0:T(4,128)(2,1)} %pix_ref.1), custom_call_target="tpu_custom_call" | custom-call | tf_op jit(solution)/shard_map/pack/pallas_call | solution.py:271
  1.8 8.4 %all-gather = bf16[128,128]{1,0:T(8,128)(2,1)S(1)} all-gather(bf16[64,128]{1,0:T(8,128)(2,1)S(1)} %get-tuple-element.45), channel_id=2, replica_groups=mesh['dp_0'=4,'dp_1'=8,'y'=8,'core'=2] {'core'}, dimensions={0}, use_global_device_ids=true | all-gather | bytes 49152 | tf_op jit(solution)/shard_map/all_gather | solution.py:289
  10.2 15.7 %conditional.1 = (bf16[32,40,128]{2,1,0:T(8,128)(2,1)}, bf16[464,1024]{1,0:T(8,128)(2,1)S(1)}) conditional(s32[]{:T(128)} %convert_element_type.3, (bf16[128,128]{1,0:T(8,128)(2,1)S(1)}, bf16[91,4,1024]{2,1,0:T(4,128)(2,1)}, f32[1024]{0:T(1024)}, f32[1024]{0:T(1024)}, bf16[91,1024]{1,0:T(8,128)(2,1)}, /*index=5*/s32[1]{0:T(128)}) %tuple.13, ...), branch_computations={%region_0.0_spmd, %region_1.0_spmd} | conditional | flops 9502720 | bytes 7151748 | solution.py:329
  10.2 0.0 copy-start.1
  10.2 0.0 copy-start.3
  10.2 0.0 copy-start.5
  10.2 0.7 %broadcast_in_dim.4 = bf16[8,2,64,128]{3,2,1,0:T(8,128)(2,1)} broadcast(bf16[2,64,128]{2,1,0:T(8,128)(2,1)S(1)} %bitcast.11), dimensions={1,2,3} | broadcast | bytes 294912 | tf_op jit(solution)/shard_map/cond/branch_0_fun/broadcast_in_dim | solution.py:317
  10.9 3.4 %all-to-all-start = ((bf16[8,2,64,128]{3,2,1,0:T(8,128)(2,1)}), bf16[8,2,64,128]{3,2,1,0:T(8,128)(2,1)S(1)}, u32[]{:S(2)}, u32[]{:S(2)}) async-start(bf16[8,2,64,128]{3,2,1,0:T(8,128)(2,1)} %broadcast_in_dim.4), calls=%async_computation | async-start | bytes 524288 | tf_op jit(solution)/shard_map/cond/branch_0_fun/all_to_all | solution.py:325
  14.4 1.5 %reshape.16.pw_ref = bf16[364,1024]{1,0:T(8,128)(2,1)S(1)} reshape(bf16[91,4,1024]{2,1,0:T(4,128)(2,1)} %get-tuple-element.29) | data formatting | bytes 1490944 | tf_op jit(solution)/shard_map/cond/branch_0_fun/reshape | solution.py:305
  15.9 0.0 copy-done.1
  15.9 0.0 copy-done.3
  15.9 0.0 copy-done.5
  15.9 1.2 %tables.2 = (bf16[464,1024]{1,0:T(8,128)(2,1)S(1)}, bf16[96,128]{1,0:T(8,128)(2,1)S(1)}) custom-call(bf16[364,1024]{1,0:T(8,128)(2,1)S(1)} %reshape.16.pw_ref, bf16[91,1024]{1,0:T(8,128)(2,1)S(1)} %copy-done.1, f32[1,1024]{1,0:T(1,128)S(1)} %bitcast.12, f32[1,1024]{1,0:T(1,128)S(1)} %bitcast.14), custom_call_target="tpu_custom_call" | custom-call | flops 9502720 | bytes 3801088 | tf_op jit(solution)/shard_map/cond/branch_0_fun/tables/pallas_call | solution.py:292
  17.1 6.5 %all-to-all-done.got_ref = bf16[8,2,64,128]{3,2,1,0:T(8,128)(2,1)S(1)} async-done(((bf16[8,2,64,128]{3,2,1,0:T(8,128)(2,1)}), bf16[8,2,64,128]{3,2,1,0:T(8,128)(2,1)S(1)}, u32[]{:S(2)}, u32[]{:S(2)}) %all-to-all-start) | async-done | bytes 262176 | tf_op jit(solution)/shard_map/cond/branch_0_fun/all_to_all | solution.py:325
  23.6 2.2 %slots.1 = bf16[1280,128]{1,0:T(8,128)(2,1)} custom-call(s32[1]{0:T(128)} %get-tuple-element.50.count_ref, bf16[8,2,64,128]{3,2,1,0:T(8,128)(2,1)S(1)} %all-to-all-done.got_ref, bf16[96,128]{1,0:T(8,128)(2,1)S(1)} %get-tuple-element.33.gram_ref), custom_call_target="tpu_custom_call" | custom-call | tf_op jit(solution)/shard_map/cond/branch_0_fun/slots/pallas_call | solution.py:318
  25.8 0.0 copy-start
  25.9 6.1 %all-gather.1 = bf16[64,40,128]{2,1,0:T(8,128)(2,1)S(1)} all-gather(bf16[32,40,128]{2,1,0:T(8,128)(2,1)} %get-tuple-element.48), channel_id=3, replica_groups=mesh['dp_0'=4,'dp_1'=8,'y'=8,'core'=2] {'core'}, dimensions={0}, use_global_device_ids=true | all-gather | bytes 983040 | tf_op jit(solution)/shard_map/all_gather | solution.py:330
  31.9 1.7 %attend.1 = bf16[16,8,128]{2,1,0:T(8,128)(2,1)S(1)} custom-call(bf16[464,1024]{1,0:T(8,128)(2,1)S(1)} %get-tuple-element.47.rows_ref, bf16[2,32,40,128]{3,2,1,0:T(8,128)(2,1)S(1)} %bitcast.9, bf16[2,1280,128]{2,1,0:T(8,128)(2,1)S(1)} %bitcast.10), custom_call_target="tpu_custom_call" | custom-call | tf_op jit(solution)/shard_map/attend/pallas_call | solution.py:332
  33.6 14.7 %all_to_all.13.m_ref = bf16[16,8,128]{2,1,0:T(8,128)(2,1)S(1)} all-to-all(bf16[16,8,128]{2,1,0:T(8,128)(2,1)S(1)} %attend.1), channel_id=1, replica_groups=mesh['dp_0'=4,'dp_1'=8,'y'=8,'core'=2] {'y','core'}, dimensions={0} | all-to-all | bytes 65536 | tf_op jit(solution)/shard_map/all_to_all | solution.py:341
  48.3 0.0 copy-done
  48.3 1.0 %project_out.1 = bf16[16,1024]{1,0:T(8,128)(2,1)} custom-call(bf16[16,8,128]{2,1,0:T(8,128)(2,1)S(1)} %all_to_all.13.m_ref, bf16[1024,1024]{1,0:T(8,128)(2,1)S(1)} %copy-done), custom_call_target="tpu_custom_call" | custom-call | tf_op jit(solution)/shard_map/project_out/pallas_call | solution.py:343
Async XLA Ops:
  10.2 5.7 %copy-start.1 = (bf16[91,1024]{1,0:T(8,128)(2,1)S(1)}, bf16[91,1024]{1,0:T(8,128)(2,1)}, u32[]{:S(2)}) copy-start(bf16[91,1024]{1,0:T(8,128)(2,1)} %get-tuple-element.30.ve_ref) | copy-start | bytes 559108 | tf_op jit(solution)/shard_map/cond
  10.2 5.7 %copy-start.3 = (f32[1024]{0:T(1024)S(1)}, f32[1024]{0:T(1024)}, u32[]{:S(2)}) copy-start(f32[1024]{0:T(1024)} %get-tuple-element.31) | copy-start | bytes 12292 | tf_op jit(solution)/shard_map/cond
  10.2 5.7 %copy-start.5 = (f32[1024]{0:T(1024)S(1)}, f32[1024]{0:T(1024)}, u32[]{:S(2)}) copy-start(f32[1024]{0:T(1024)} %get-tuple-element.32) | copy-start | bytes 12292 | tf_op jit(solution)/shard_map/cond
  10.9 12.7 %all-to-all-start = ((bf16[8,2,64,128]{3,2,1,0:T(8,128)(2,1)}), bf16[8,2,64,128]{3,2,1,0:T(8,128)(2,1)S(1)}, u32[]{:S(2)}, u32[]{:S(2)}) async-start(bf16[8,2,64,128]{3,2,1,0:T(8,128)(2,1)} %broadcast_in_dim.4), calls=%async_computation | async-start | bytes 524288 | tf_op jit(solution)/shard_map/cond/branch_0_fun/all_to_all | solution.py:325
  25.8 22.4 %copy-start = (bf16[1024,1024]{1,0:T(8,128)(2,1)S(1)}, bf16[1024,1024]{1,0:T(8,128)(2,1)}, u32[]{:S(2)}) copy-start(bf16[1024,1024]{1,0:T(8,128)(2,1)} %wo_ref.1) | copy-start | bytes 6291460
